TPU v7x, 128 devices: a whole 4x4x4 slice. The times are simulated.
128 devices in a mesh: row: 8 (over x, core), col: 16 (over y, z).
Axes of the slice: x: 4, y: 4, z: 4, core: 2. Of those that a mesh axis runs over, the one named last changes fastest.
Arguments:
- valence: bfloat16 [2, 16, 32768], replicated, may hold values from -6 to 6
- conduction: bfloat16 [2, 128, 32768], replicated, may hold values from -6 to 6
- valence_energy: float32 [16], replicated, may hold values from -8 to -1
- conduction_energy: float32 [128], replicated, may hold values from 0.5 to 6
- band_pairs: int32 [1024, 2], P(('row', 'col')), may hold values from 0 to 127, as said below
- grid_index: int32 [16384], replicated, may hold values from 0 to 32767, as said below
Outputs:
- response: float32 [2, 16384, 16384], P(None, 'row', 'col')
Inputs may be any that keep to these rules, and one draw needn't show every extreme that they name: `band_pairs`: the rows are distinct combinations of a valence band below 16 and a conduction band below 128, half of all combinations. `grid_index`: the 16384 entries are distinct.
All inputs are finite; a program needn't handle non-finite values.
Results may differ from a plain program's by a relative error of at most 0.0039.
Values may be sent and summed in bfloat16 or wider, within the bound.
A program may use at most 192 MiB of HBM per device.

v0:
```python
import math

import jax
import jax.numpy as jnp
from jax import lax
from jax.sharding import PartitionSpec as P

N1 = 32
N2 = 32
N3 = 32
NVB = 16
NCB = 128


def tables(length):
    position = jnp.arange(length, dtype=jnp.int32)
    phase_angle = (position[:, None] * position[None, :] % length).astype(jnp.float32) * (
        2.0 * math.pi / length
    )
    return (jnp.cos(phase_angle), jnp.sin(phase_angle))


def plane_table():
    plane_size = N2 * N3
    position = jnp.arange(plane_size, dtype=jnp.int32)
    second = position // N3
    third = position % N3
    phase_index = (
        second[:, None] * second[None, :] % N2 * N3 + third[:, None] * third[None, :] % N3 * N2
    )
    phase_angle = (phase_index % plane_size).astype(jnp.float32) * (2.0 * math.pi / plane_size)
    cosine = jnp.cos(phase_angle)
    sine_table = jnp.sin(phase_angle)
    upper = jnp.concatenate([cosine, -sine_table], axis=1)
    lower = jnp.concatenate([sine_table, cosine], axis=1)
    return jnp.concatenate([upper, lower], axis=0)


def transform(rho_real, rho_imag):
    pair_count = rho_real.shape[0]
    plane_size = N2 * N3
    stacked = jnp.concatenate(
        [
            rho_real.reshape(pair_count, N1, plane_size),
            rho_imag.reshape(pair_count, N1, plane_size),
        ],
        axis=2,
    )
    plane = jnp.dot(
        stacked.reshape(pair_count * N1, 2 * plane_size),
        plane_table(),
        precision=lax.Precision.HIGHEST,
    )
    plane = plane.reshape(pair_count, N1, 2 * plane_size)
    cosine, sine_table = tables(N1)
    cos_part = jnp.einsum("kr,prx->pkx", cosine, plane, precision=lax.Precision.HIGHEST)
    sin_part = jnp.einsum("kr,prx->pkx", sine_table, plane, precision=lax.Precision.HIGHEST)
    out_real = cos_part[:, :, :plane_size] + sin_part[:, :, plane_size:]
    out_imag = cos_part[:, :, plane_size:] - sin_part[:, :, :plane_size]
    return (out_real.reshape(pair_count, -1), out_imag.reshape(pair_count, -1))


def pair_spectrum(valence, conduction, valence_energy, conduction_energy, band_pairs):
    valence_rows = jnp.take(valence, band_pairs[:, 0], axis=1).astype(jnp.float32)
    conduction_rows = jnp.take(conduction, band_pairs[:, 1], axis=1).astype(jnp.float32)
    rho_real = valence_rows[0] * conduction_rows[0] + valence_rows[1] * conduction_rows[1]
    rho_imag = valence_rows[0] * conduction_rows[1] - valence_rows[1] * conduction_rows[0]
    out_real, out_imag = transform(rho_real, rho_imag)
    normalize = 1.0 / math.sqrt(N1 * N2 * N3)
    spectrum = jnp.stack([out_real, out_imag]) * normalize
    valence_hot = (
        band_pairs[:, 0][:, None] == jnp.arange(valence_energy.shape[0], dtype=jnp.int32)[None, :]
    )
    conduction_hot = (
        band_pairs[:, 1][:, None]
        == jnp.arange(conduction_energy.shape[0], dtype=jnp.int32)[None, :]
    )
    energy_gap = jnp.sum(jnp.where(valence_hot, valence_energy[None, :], 0.0), axis=1) - jnp.sum(
        jnp.where(conduction_hot, conduction_energy[None, :], 0.0), axis=1
    )
    weights = 2.0 / (math.sqrt(NVB * NCB // 2) * energy_gap)
    return (spectrum, weights)


def contract(weighted_part, operand, left_dims, right_dims):
    full_left = (0,) + tuple((d + 1 for d in left_dims))
    full_right = (0,) + tuple((d + 1 for d in right_dims))
    real_part = lax.dot_general(
        weighted_part,
        operand,
        ((full_left, full_right), ((), ())),
        preferred_element_type=jnp.float32,
    )
    pair_dims = ((left_dims, right_dims), ((), ()))
    imag_part = lax.dot_general(
        weighted_part[0], operand[1], pair_dims, preferred_element_type=jnp.float32
    ) - lax.dot_general(weighted_part[1], operand[0], pair_dims, preferred_element_type=jnp.float32)
    return jnp.stack([real_part, imag_part])


def body(valence, conduction, valence_energy, conduction_energy, band_pairs, grid_index):
    spectrum, weights = pair_spectrum(
        valence, conduction, valence_energy, conduction_energy, band_pairs
    )
    row_count = lax.axis_size("row")
    column_count = lax.axis_size("col")
    selected = jnp.take(spectrum, grid_index, axis=2)
    weighted = (weights[None, :, None] * selected).astype(jnp.bfloat16)
    density = selected.astype(jnp.bfloat16)
    weighted_block = lax.all_to_all(weighted, "row", split_axis=2, concat_axis=1, tiled=True)
    density_block = lax.all_to_all(density, "col", split_axis=2, concat_axis=1, tiled=True)
    weighted_all = lax.all_gather(weighted_block, "col", axis=1, tiled=True)
    density_all = lax.all_gather(density_block, "row", axis=1, tiled=True)
    pair_count = density_all.shape[1]
    per_device = pair_count // (row_count * column_count)
    weighted_split = weighted_all.reshape(
        2, column_count, row_count, per_device, weighted_all.shape[2]
    )
    density_split = density_all.reshape(
        2, row_count, column_count, per_device, density_all.shape[2]
    )
    return contract(weighted_split, density_split, (0, 1, 2), (1, 0, 2))


def solution(mesh):
    return jax.shard_map(
        body,
        mesh=mesh,
        in_specs=(P(), P(), P(), P(), P(("row", "col"), None), P()),
        out_specs=P(None, "row", "col"),
        check_vma=False,
    )
```

profile of v0, /device:TPU:0, one launch (start us, length us, event | category | flops | bytes accessed | tf_op | source)
XLA Modules:
  0.0 723.4 jit_solution(14251131210681987142)
XLA Ops:
  6.5 0.8 fusion.55
  8.2 3.6 gather_fusion.1
  11.8 1.5 convert_bitcast_fusion.1
  13.3 3.5 gather_fusion
  17.1 1.4 copy-done.2
  20.0 23.7 %fusion.25 = (f32[1024,1024]{1,0:T(8,128)}, f32[1024,1024]{1,0:T(8,128)}, f32[1024,1024]{1,0:T(8,128)}) fusion(s32[1024]{0:T(1024)S(1)} %get-tuple-element.24, s32[1024]{0:T(1024)S(1)} %get-tuple-element.25), kind=kLoop, calls=%fused_computation.53 | loop fusion | flops 41943040 | bytes 12591104 | tf_op jit(solution)/shard_map/neg | solution.py:34
  43.7 22.3 %fusion = f32[8,32,2048]{2,1,0:T(8,128)} fusion(f32[1024,1024]{1,0:T(8,128)} %get-tuple-element.15, f32[1024,1024]{1,0:T(8,128)} %get-tuple-element.14, f32[1024,1024]{1,0:T(8,128)} %get-tuple-element.13, f32[8,32,1024]{2,1,0:T(8,128)S(1)} %bitcast.102, f32[8,32,1024]{2,1,0:T(8,128)S(1)} %bitcast.103), kind=kOutput, calls=%fused_computation.4 | convolution fusion | flops 12898009088 | bytes 16777216 | tf_op jit(solution)/shard_map/dot_general | solution.py:49
  66.0 3.8 convolution_bitcast_fusion.1
  69.9 2.1 convolution_bitcast_fusion.2
  72.0 1.4 slice_add_fusion
  73.4 2.4 stack_reshape.6
  75.8 1.2 stack_reshape.7
  77.0 1.7 maximum_multiply_fusion
  78.7 28.8 %copy.31 = f32[2,8,32768]{1,0,2:T(2,128)} copy(f32[2,8,32768]{2,1,0:T(8,128)S(1)} %maximum_multiply_fusion) | data formatting | bytes 4194304 | tf_op jit(solution)/shard_map/mul | solution.py:70
  107.5 252.0 %gather_fusion.2 = f32[16384,2,8]{2,1,0:T(2,128)} fusion(f32[2,8,32768]{1,0,2:T(2,128)} %copy.31, s32[16384]{0:T(1024)S(1)} %fusion.26), kind=kCustom, calls=%fused_computation.2 | custom fusion | bytes 2162688 | tf_op jit(solution)/shard_map/jit(_take)/gather | solution.py:107
  359.5 71.1 %fusion.59 = bf16[16384,2,8]{2,1,0:T(2,128)(2,1)} fusion(f32[16384,2,8]{2,1,0:T(2,128)} %gather_fusion.2, pred[16384]{0:T(1024)(128)(4,1)S(1)} %compare_and_fusion), kind=kLoop, calls=%fused_computation.113 | loop fusion | flops 262144 | bytes 1589248
  430.6 10.5 %reshape.154 = bf16[16,2,8192]{2,1,0:T(2,128)(2,1)S(1)} reshape(bf16[16384,2,8]{2,1,0:T(2,128)(2,1)} %fusion.59) | data formatting | bytes 1048576
  441.1 19.4 %all_to_all.36 = bf16[16,2,8192]{2,1,0:T(2,128)(2,1)S(1)} all-to-all(bf16[16,2,8192]{2,1,0:T(2,128)(2,1)S(1)} %reshape.154), channel_id=1, replica_groups=mesh['row'=8,'col'=16] {'col'}, dimensions={0} | all-to-all | bytes 1048576 | tf_op jit(solution)/shard_map/all_to_all | solution.py:111
  460.5 10.9 %reshape.155 = bf16[16384,2,8]{2,1,0:T(2,128)(2,1)} reshape(bf16[16,2,8192]{2,1,0:T(2,128)(2,1)S(1)} %all_to_all.36) | data formatting | bytes 1048576
  471.4 19.3 %copy.33 = bf16[2,16,8,1024]{3,2,1,0:T(8,128)(2,1)} copy(bf16[2,16,8,1024]{2,0,3,1:T(2,128)(2,1)} %bitcast.90) | data formatting | bytes 1048576 | tf_op jit(solution)/shard_map/all_to_all | solution.py:111
  491.1 59.2 %fusion.60 = bf16[16384,2,8]{2,1,0:T(2,128)(2,1)} fusion(f32[16384,2,8]{2,1,0:T(2,128)} %gather_fusion.2, pred[16384]{0:T(1024)(128)(4,1)S(1)} %compare_and_fusion, f32[8]{0:T(128)S(1)} %multiply_divide_fusion), kind=kLoop, calls=%fused_computation.114 | loop fusion | flops 786432 | bytes 1589280
  550.3 10.4 %reshape.152 = bf16[8,2,16384]{2,1,0:T(2,128)(2,1)S(1)} reshape(bf16[16384,2,8]{2,1,0:T(2,128)(2,1)} %fusion.60) | data formatting | bytes 1048576
  560.7 14.5 %all_to_all.37 = bf16[8,2,16384]{2,1,0:T(2,128)(2,1)S(1)} all-to-all(bf16[8,2,16384]{2,1,0:T(2,128)(2,1)S(1)} %reshape.152), channel_id=1, replica_groups=mesh['row'=8,'col'=16] {'row'}, dimensions={0} | all-to-all | bytes 1048576 | tf_op jit(solution)/shard_map/all_to_all | solution.py:110
  575.2 10.9 %reshape.153 = bf16[16384,2,8]{2,1,0:T(2,128)(2,1)} reshape(bf16[8,2,16384]{2,1,0:T(2,128)(2,1)S(1)} %all_to_all.37) | data formatting | bytes 1048576
  586.1 19.2 %copy.32 = bf16[2,8,8,2048]{3,2,1,0:T(8,128)(2,1)} copy(bf16[2,8,8,2048]{2,0,3,1:T(2,128)(2,1)} %bitcast.91) | data formatting | bytes 1048576 | tf_op jit(solution)/shard_map/all_to_all | solution.py:110
  605.3 4.7 fusion.58
  610.0 62.3 %all-gather.3.cloned.1.call-done = bf16[2,1024,2048]{2,1,0:T(8,128)(2,1)} async-done(((bf16[2,64,2048]{2,1,0:T(8,128)(2,1)}), bf16[2,1024,2048]{2,1,0:T(8,128)(2,1)}) %all-gather.3.cloned.1.call-update) | async-done | bytes 8388624 | tf_op jit(solution)/shard_map/all_gather | solution.py:112
  672.3 14.5 %convolution_bitcast_fusion = f32[1,2048,1024]{2,1,0:T(8,128)} fusion(bf16[2,16,8,8,2048]{4,3,2,1,0:T(8,128)(2,1)} %bitcast.92, bf16[2,8,16,8,1024]{4,3,2,1,0:T(8,128)(2,1)} %bitcast.93), kind=kOutput, calls=%fused_computation.31 | convolution fusion | flops 8589934592 | bytes 20971520 | tf_op jit(solution)/shard_map/dot_general | solution.py:88
  686.8 5.4 fusion.57
  692.2 6.9 fusion.21
  699.1 7.4 %fusion.8 = f32[1,2048,1024]{2,1,0:T(8,128)S(1)} fusion(f32[2048,1024,1,1]{1,0,3,2:T(8,128)} %fusion.21, bf16[16,8,8,2048]{3,2,1,0:T(8,128)(2,1)S(1)} %bitcast.96, bf16[8,16,8,1024]{3,2,1,0:T(8,128)(2,1)S(1)} %bitcast.100), kind=kOutput, calls=%fused_computation.16 | convolution fusion | flops 4297064448 | bytes 23068672 | tf_op jit(solution)/shard_map/dot_general | solution.py:97
  706.5 10.0 %pad_maximum_fusion = f32[2,2048,1024]{2,1,0:T(8,128)} fusion(f32[1,2048,1024]{2,1,0:T(8,128)S(1)} %fusion.8, f32[1,2048,1024]{2,1,0:T(8,128)} %convolution_bitcast_fusion), kind=kLoop, calls=%fused_computation.11 | loop fusion | flops 4194304 | bytes 33554432 | tf_op jit(solution)/shard_map/stack | solution.py:98
  (36 shorter events, 3.1 us)
Async XLA Ops:
  6.5 6.8 copy-start
  6.5 598.8 %all-gather.5.cloned.1.call-start = ((), (), s32[]{:S(2)}) async-start(), calls=%async_computation.3 | async-start | bytes 4718592 | tf_op jit(solution)/shard_map/all_gather | solution.py:113
  16.9 1.6 copy-start.2
  66.0 3.8 copy-start.3
  66.0 6.0 copy-start.7
  471.4 19.3 %copy-start.8 = (f32[128]{0:T(128)S(1)}, f32[128]{0:T(128)}, u32[]{:S(2)}) copy-start(f32[128]{0:T(128)} %param.9) | copy-start | bytes 1540
  471.4 19.5 %copy-start.9 = (f32[16]{0:T(128)S(1)}, f32[16]{0:T(128)}, u32[]{:S(2)}) copy-start(f32[16]{0:T(128)} %param.8) | copy-start | bytes 196
  490.7 181.6 %all-gather.3.cloned.1.call-start = ((), (), s32[]{:S(2)}) async-start(), calls=%async_computation.2 | async-start | bytes 8912896 | tf_op jit(solution)/shard_map/all_gather | solution.py:112
  686.8 5.4 copy-start.6
  692.2 7.0 copy-start.4
  692.2 7.0 copy-start.5
  706.5 10.0 %copy-start.1 = (bf16[2,16,32768]{2,1,0:T(8,128)(2,1)S(1)}, bf16[2,16,32768]{2,1,0:T(8,128)(2,1)}, u32[]{:S(2)}) copy-start(bf16[2,16,32768]{2,1,0:T(8,128)(2,1)} %param.6) | copy-start | bytes 6291460
Sparse Core Ops, SparseCore 0:
  490.8 29.8 all-gather.4
  605.4 66.8 all-gather.2
where the time goes:
time: 734 us; the launch traced here: 723 us
  local copies, waits for them, and re-layouts  385 us (52%)
  other arithmetic  171 us (23%)
  waiting for transfers between devices  62.4 us (9%)
  matrix products  57 us (8%)
  blocking collectives  33.9 us (5%)
  between operations  13.6 us (2%)
    gather x1, local copies, waits for them, and re-layouts, body(): selected = jnp.take(spectrum, grid_index, axis=2)  252 us
    unnamed x2, other arithmetic  130 us
    all_gather x1, waiting for transfers between devices, body(): weighted_all = lax.all_gather(weighted_block, 'col', axis=1, tiled=True)  62.3 us
    unnamed x26, local copies, waits for them, and re-layouts  45.3 us
    mul x1, local copies, waits for them, and re-layouts, pair_spectrum(): spectrum = jnp.stack([out_real, out_imag]) * normalize  28.8 us
    neg x1, other arithmetic, plane_table(): upper = jnp.concatenate([cosine, -sine_table], axis=1)  23.7 us
    dot_general x1, matrix products, transform(): jnp.dot(stacked.reshape(pair_count * N1, 2 * plane_size), plane_table(),...  22.3 us
    all_to_all x1, blocking collectives, body(): lax.all_to_all(density, 'col', split_axis=2, concat_axis=1, tiled=True)  19.4 us
  transfers between devices with their start and end apart: 2, of which 1 were waited for; matrix products, arithmetic and copies ran while one was open for 14% of the time, Pallas kernels for 0%

commit v1 on v0

v1 whole, which is shorter than its diff:
```python
import math
import numpy as np
import jax
import jax.numpy as jnp
import ml_dtypes
from jax import lax
from jax.sharding import PartitionSpec as P
from jax.experimental import pallas as pl
from jax.experimental.pallas import tpu as pltpu

N1 = N2 = N3 = 32
KA, KB = 256, 128
NGV = 16384
GW = 512


def split_np(t):
    hi = t.astype(ml_dtypes.bfloat16)
    lo = (t - hi.astype(np.float64)).astype(ml_dtypes.bfloat16)
    return hi, lo


def dft_tables():
    a = np.arange(KA)
    r1, r2a = a // 8, a % 8
    ph = (np.outer(r1, r1) / 32.0 + np.outer(r2a, r2a) / 8.0) % 1.0
    c, s = np.cos(2 * np.pi * ph), np.sin(2 * np.pi * ph)
    ta = np.block([[c, s], [-s, c]])
    b = np.arange(KB)
    r2b, r3 = b // 32, b % 32
    ph = (np.outer(r2b, r2b) / 4.0 + np.outer(r3, r3) / 32.0) % 1.0
    c, s = np.cos(2 * np.pi * ph), np.sin(2 * np.pi * ph)
    tb = np.block([[c, s], [-s, c]])
    ph = np.outer(r2a, r2b) / 32.0
    tw = np.stack([np.cos(2 * np.pi * ph), np.sin(2 * np.pi * ph)]).astype(np.float32)
    ta_hi, ta_lo = split_np(ta)
    tb_hi, tb_lo = split_np(tb)
    fold = np.zeros((16, 128), ml_dtypes.bfloat16)
    for p in range(8):
        for ri in range(2):
            fold[ri * 8 + p, p * 16 + ri * 8 : p * 16 + ri * 8 + 8] = 1
    return np.stack([ta_hi, ta_lo]), np.stack([tb_hi, tb_lo]), tw, fold


def split(x):
    hi = x.astype(jnp.bfloat16)
    return hi, (x - hi.astype(jnp.float32)).astype(jnp.bfloat16)


def dot_f32(a, b, dims):
    return lax.dot_general(a, b, (dims, ((), ())), preferred_element_type=jnp.float32)


def spectrum_kernel(v_ref, c_ref, scale_ref, index_ref, ta_ref, tb_ref, tw_ref, fold_ref, y_ref, rr, ri, xt):
    def products(a, _):
        lanes = pl.ds(pl.multiple_of(a * 128, 128), 128)
        vr, vi = v_ref[0, :, lanes].astype(jnp.float32), v_ref[1, :, lanes].astype(jnp.float32)
        cr, ci = c_ref[0, :, lanes].astype(jnp.float32), c_ref[1, :, lanes].astype(jnp.float32)
        rows = pl.ds(pl.multiple_of(a * 8, 8), 8)
        rr[rows, :] = vr * cr + vi * ci
        ri[rows, :] = vr * ci - vi * cr
        return 0

    lax.fori_loop(0, KA, products, 0, unroll=8)

    nn = ((1,), (0,))
    nt = ((1,), (1,))
    for h in range(4):
        x = jnp.concatenate(
            [
                jnp.concatenate([r[pl.ds(2 * h + q, KA, stride=8), :] for q in range(2)], axis=1)
                for r in (rr, ri)
            ],
            axis=0,
        )
        xh, xl = split(x)
        z = dot_f32(ta_ref[0], xh, nn) + (dot_f32(ta_ref[0], xl, nn) + dot_f32(ta_ref[1], xh, nn))
        for q in range(2):
            p = 2 * h + q
            zr, zi = z[:KA, q * KB : (q + 1) * KB], z[KA:, q * KB : (q + 1) * KB]
            t = jnp.concatenate([zr * tw_ref[0] + zi * tw_ref[1], zi * tw_ref[0] - zr * tw_ref[1]], axis=1)
            th, tl = split(t)
            s = dot_f32(tb_ref[0], th, nt) + (dot_f32(tb_ref[0], tl, nt) + dot_f32(tb_ref[1], th, nt))
            xt[p] = (s * scale_ref[p]).astype(jnp.bfloat16)

    def select(w, _):
        k = index_ref[pl.ds(w, 1), :]
        ka = (k >> 10) * 8 + ((k >> 5) & 7)
        kb = ((k >> 8) & 3) * 32 + (k & 31)
        hot = jnp.where(lax.broadcasted_iota(jnp.int32, (KA, GW), 0) == ka, 1.0, 0.0).astype(jnp.bfloat16)
        kb_hi = jnp.broadcast_to(kb >> 3, (8, GW))
        low = lax.broadcasted_iota(jnp.int32, (8, GW), 0) == (kb & 7)
        parts = []
        for p in range(8):
            r = jnp.dot(xt[p], hot, preferred_element_type=jnp.float32)
            for q in range(2):
                acc = r[q * KB : q * KB + 8]
                for j in range(1, 16):
                    acc = jnp.where(kb_hi == j, r[q * KB + j * 8 : q * KB + j * 8 + 8], acc)
                parts.append(jnp.where(low, acc, 0.0))
        part = jnp.concatenate(parts, axis=0).astype(jnp.bfloat16)
        y = jnp.dot(fold_ref[...], part, preferred_element_type=jnp.float32)
        y_ref[:, pl.ds(pl.multiple_of(w * GW, GW), GW)] = y.astype(jnp.bfloat16)
        return 0

    lax.fori_loop(0, NGV // GW, select, 0)


def spectrum(v_rows, c_rows, scale, index):
    ta, tb, tw, fold = dft_tables()
    vm = pl.BlockSpec(memory_space=pltpu.VMEM)
    return pl.pallas_call(
        spectrum_kernel,
        out_shape=jax.ShapeDtypeStruct((16, NGV), jnp.bfloat16),
        in_specs=[vm, vm, pl.BlockSpec(memory_space=pltpu.SMEM)] + [vm] * 5,
        out_specs=vm,
        scratch_shapes=[
            pltpu.VMEM((8 * KA, 128), jnp.float32),
            pltpu.VMEM((8 * KA, 128), jnp.float32),
            pltpu.VMEM((8, 256, 256), jnp.bfloat16),
        ],
        compiler_params=pltpu.CompilerParams(vmem_limit_bytes=48 << 20),
        name="spectrum",
    )(v_rows, c_rows, scale, index.reshape(NGV // GW, GW), jnp.asarray(ta), jnp.asarray(tb), jnp.asarray(tw), jnp.asarray(fold))


MESH = pl.DeviceIdType.MESH
ROWS, COLS = 8, 16
GA, GB = NGV // ROWS, NGV // COLS
HALF, PART = GA // 2, GA // 4


def exchange_kernel(y_ref, a_ref, b_ref, pa, at, send, recv, local):
    row, col = lax.axis_index("row"), lax.axis_index("col")
    x, core = row // 2, row % 2
    py, pz = col // 4, col % 4

    def cell(dy, dz):
        return lax.rem(py + dy + 4, 4) * 4 + lax.rem(pz + dz + 4, 4)

    def line(dx, dc=0):
        return lax.rem(x + dx + 4, 4) * 2 + lax.rem(core + dc, 2)

    started = []

    def remote(k, src, dst, device):
        copy = pltpu.make_async_remote_copy(
            src_ref=src, dst_ref=dst, send_sem=send.at[k], recv_sem=recv.at[k],
            device_id=device, device_id_type=MESH,
        )
        copy.start()
        started.append(copy)

    def arrived(k, dst):
        pltpu.make_async_remote_copy(
            src_ref=dst, dst_ref=dst, send_sem=send.at[k], recv_sem=recv.at[k],
            device_id=(row, col), device_id_type=MESH,
        ).wait_recv()

    barrier = pltpu.get_barrier_semaphore()
    for d in range(1, ROWS):
        pl.semaphore_signal(barrier, inc=1, device_id=(lax.rem(row + d, ROWS), col), device_id_type=MESH)
    for d in range(1, COLS):
        pl.semaphore_signal(barrier, inc=1, device_id=(row, lax.rem(col + d, COLS)), device_id_type=MESH)
    pl.semaphore_wait(barrier, ROWS + COLS - 2)

    def a_cols(i):
        return y_ref.at[:, pl.ds(pl.multiple_of(i * GA, GA), GA)]

    def b_cols(j):
        return y_ref.at[:, pl.ds(pl.multiple_of(j * GB, GB), GB)]

    own_a = pltpu.make_async_copy(a_cols(row), pa.at[row], local.at[0])
    own_a.start()
    for d in range(1, ROWS):
        to = lax.rem(row + d, ROWS)
        remote(d - 1, a_cols(to), pa.at[row], (to, col))
    own_b = pltpu.make_async_copy(b_cols(col), b_ref.at[row, col], local.at[1])
    own_b.start()
    base_b0 = 7
    for d in range(1, COLS):
        to = lax.rem(col + d, COLS)
        remote(base_b0 + d - 1, b_cols(to), b_ref.at[row, col], (row, to))

    own_a.wait()
    for d in range(1, ROWS):
        arrived(d - 1, pa.at[lax.rem(row - d + ROWS, ROWS)])

    base_a = (22, 42)

    def turn(h):
        def step(n, _):
            cols = pl.ds(pl.multiple_of(h * HALF + n * 128, 128), 128)
            block = pa[:, :, cols].reshape(128, 128)
            at[cols, :] = block.astype(jnp.float32).T.astype(jnp.bfloat16)
            return 0

        lax.fori_loop(0, HALF // 128, step, 0)

    def near(h, s, d):
        on_y = (h == 0) == (s == 0)
        return cell(d, 0) if on_y else cell(0, d)

    def offset(h, u, d):
        return cell(u, d) if h == 0 else cell(d, u)

    def rows_of(h, part=None):
        if part is None:
            return pl.ds(h * HALF, HALF)
        return pl.ds(h * HALF + part * PART, PART)

    def chunk(h, j, part=None):
        return a_ref.at[j, rows_of(h, part)]

    own_copies = []
    for h in range(2):
        turn(h)
        mine = at.at[rows_of(h)]
        for n, d in ((0, 1), (1, -1)):
            remote(base_a[h] + n, mine, chunk(h, col), (row, near(h, 0, d)))
        copy = pltpu.make_async_copy(mine, chunk(h, col), local.at[2 + h])
        copy.start()
        own_copies.append(copy)

    def second(h, slot, u):
        j = offset(h, u, 0)
        src = at.at[rows_of(h)] if u == 0 else chunk(h, j)
        for n, d in ((0, 1), (1, -1)):
            remote(base_a[h] + 4 + slot * 4 + n, src, chunk(h, j), (row, near(h, 1, d)))

    for h in range(2):
        second(h, 0, 0)

    base_b1 = 62
    own_b.wait()
    for d in range(1, COLS):
        arrived(base_b0 + d - 1, b_ref.at[row, lax.rem(col - d + COLS, COLS)])
    remote(base_b1 + 0, b_ref.at[row], b_ref.at[row], (line(1), col))
    remote(base_b1 + 1, b_ref.at[row], b_ref.at[row], (line(-1), col))
    remote(base_b1 + 2, b_ref.at[row], b_ref.at[row], (line(0, 1), col))

    def b_part(i, part):
        return b_ref.at[i, pl.ds(part * 8, 8)]

    for n, d in ((0, -1), (1, 1)):
        for h in range(2):
            j = offset(h, d, 0)
            arrived(base_a[h] + n, chunk(h, j))
            remote(base_a[h] + 2 + n, chunk(h, j, n), chunk(h, j, n), (row, near(h, 0, -d)))
            second(h, 1 + n, d)

    for n, d in ((0, -1), (1, 1)):
        i = line(d)
        arrived(base_b1 + n, b_ref.at[i])
        remote(base_b1 + 3 + n, b_part(i, n), b_part(i, n), (line(-d), col))
        remote(base_b1 + 5 + n, b_ref.at[i], b_ref.at[i], (line(0, 1), col))

    for h in range(2):
        j = offset(h, 2, 0)
        for n in range(2):
            arrived(base_a[h] + 2 + n, chunk(h, j, n))
        second(h, 3, 2)

    for n in range(2):
        arrived(base_b1 + 3 + n, b_part(line(2), n))
        remote(base_b1 + 7 + n, b_part(line(2), n), b_part(line(2), n), (line(0, 1), col))

    for slot, u in enumerate((0, -1, 1, 2)):
        for n, d in ((0, -1), (1, 1)):
            for h in range(2):
                j = offset(h, u, d)
                k = base_a[h] + 4 + slot * 4
                arrived(k + n, chunk(h, j))
                remote(k + 2 + n, chunk(h, j, n), chunk(h, j, n), (row, near(h, 1, -d)))
    for slot, u in enumerate((0, -1, 1, 2)):
        for n in range(2):
            for h in range(2):
                arrived(base_a[h] + 4 + slot * 4 + 2 + n, chunk(h, offset(h, u, 2), n))

    arrived(base_b1 + 2, b_ref.at[line(0, 1)])
    for n, d in ((0, -1), (1, 1)):
        arrived(base_b1 + 5 + n, b_ref.at[line(d, 1)])
        arrived(base_b1 + 7 + n, b_part(line(2, 1), n))
    for copy in own_copies:
        copy.wait()
    for copy in started:
        copy.wait_send()


def exchange(y):
    anywhere = pl.BlockSpec(memory_space=pl.ANY)
    return pl.pallas_call(
        exchange_kernel,
        out_shape=(
            jax.ShapeDtypeStruct((COLS, GA, 128), jnp.bfloat16),
            jax.ShapeDtypeStruct((ROWS, COLS, 16, GB), jnp.bfloat16),
        ),
        in_specs=[anywhere],
        out_specs=(anywhere, anywhere),
        scratch_shapes=[
            pltpu.VMEM((ROWS, 16, GA), jnp.bfloat16),
            pltpu.VMEM((GA, 128), jnp.bfloat16),
            pltpu.SemaphoreType.DMA((71,)),
            pltpu.SemaphoreType.DMA((71,)),
            pltpu.SemaphoreType.DMA((4,)),
        ],
        compiler_params=pltpu.CompilerParams(collective_id=0, has_side_effects=True),
        name="exchange",
    )(y)


TM = 256


def response_kernel(a_ref, b_ref, o_ref, rhs):
    @pl.when(pl.program_id(0) == 0)
    def _():
        def build(n, _):
            i, j = n // COLS, lax.rem(n, COLS)
            block = b_ref[i, j].astype(jnp.float32)
            re, im = block[:8], block[8:]
            rows = pl.ds(pl.multiple_of(j * 128 + i * 16, 16), 16)
            rhs[rows, :GB] = (-block).astype(jnp.bfloat16)
            rhs[rows, GB:] = jnp.concatenate([-im, re], axis=0).astype(jnp.bfloat16)
            return 0

        lax.fori_loop(0, ROWS * COLS, build, 0)

    lhs = jnp.concatenate([a_ref[j] for j in range(COLS)], axis=1)
    for q in range(2):
        o_ref[q] = jnp.dot(lhs, rhs[:, q * GB : (q + 1) * GB], preferred_element_type=jnp.float32)


def contract(a, b):
    return pl.pallas_call(
        response_kernel,
        out_shape=jax.ShapeDtypeStruct((2, GA, GB), jnp.float32),
        grid=(GA // TM,),
        in_specs=[
            pl.BlockSpec((COLS, TM, 128), lambda m: (0, m, 0)),
            pl.BlockSpec((ROWS, COLS, 16, GB), lambda m: (0, 0, 0, 0), pipeline_mode=pl.Buffered(1)),
        ],
        out_specs=pl.BlockSpec((2, TM, GB), lambda m: (0, m, 0)),
        scratch_shapes=[pltpu.VMEM((COLS * 128, 2 * GB), jnp.bfloat16)],
        compiler_params=pltpu.CompilerParams(vmem_limit_bytes=48 << 20),
        name="contract",
    )(a, b)


def body(valence, conduction, valence_energy, conduction_energy, band_pairs, grid_index):
    v, c = band_pairs[:, 0], band_pairs[:, 1]
    v_rows = jnp.take(valence, v, axis=1, mode="clip")
    c_rows = jnp.take(conduction, c, axis=1, mode="clip")
    gap = jnp.take(valence_energy, v, mode="clip") - jnp.take(conduction_energy, c, mode="clip")
    scale = jnp.sqrt(-2.0 / (math.sqrt(1024) * gap)) / math.sqrt(N1 * N2 * N3)
    y = spectrum(v_rows, c_rows, scale, grid_index)
    a, b = exchange(y)
    return contract(a, b)


def solution(mesh):
    return jax.shard_map(
        body,
        mesh=mesh,
        in_specs=(P(), P(), P(), P(), P(("row", "col"), None), P()),
        out_specs=P(None, "row", "col"),
        check_vma=False,
    )
```

time: 734 us -> 142 us (0.19); the launches traced: 723 us -> 141 us
  local copies, waits for them, and re-layouts: 385 us -> 18.8 us
  other arithmetic: 171 us -> 0.02 us
  Pallas kernels: 0 us -> 122 us
  waiting for transfers between devices: 62.4 us -> 0 us
  matrix products: 57 us -> 0 us
  blocking collectives: 33.9 us -> 0 us
  between operations: 13.6 us -> 0.07 us
    gather x3 -> x4, local copies, waits for them, and re-layouts: 259 us -> 10.7 us  [the longest x1 4.58 us: body(): c_rows = jnp.take(conduction, c, axis=1, mode='clip')]
    unnamed x2 -> x0, other arithmetic: 130 us -> none
    pallas_call x0 -> x3, Pallas kernels: none -> 122 us  [the longest x1 65 us: exchange(): pl.pallas_call(exchange_kernel, out_shape=(jax.ShapeDtypeStruct((COLS, GA...]
    all_gather x2 -> x0, waiting for transfers between devices: 62.3 us -> none  [the longest x1 62.3 us: body(): weighted_all = lax.all_gather(weighted_block, 'col', axis=1, tiled=True)]
    dot_general x6 -> x0, matrix products: 57 us -> none  [the longest x1 22.3 us: transform(): jnp.dot(stacked.reshape(pair_count * N1, 2 * plane_size), plane_table(),...]
    unnamed x26 -> x16, local copies, waits for them, and re-layouts: 45.3 us -> 6.39 us
    all_to_all x2 -> x0, local copies, waits for them, and re-layouts: 38.4 us -> none  [the longest x1 19.3 us: body(): lax.all_to_all(density, 'col', split_axis=2, concat_axis=1, tiled=True)]
    all_to_all x2 -> x0, blocking collectives: 33.9 us -> none  [the longest x1 19.4 us: body(): lax.all_to_all(density, 'col', split_axis=2, concat_axis=1, tiled=True)]
  transfers between devices with their start and end apart: 2 -> 0, of which waited for: 1 -> 0; matrix products, arithmetic and copies ran while one was open for 14% -> 0% of each run, Pallas kernels for 0% -> 0%
where the time goes in v1:
time: 142 us; the launch traced here: 141 us
  Pallas kernels  122 us (86%)
  local copies, waits for them, and re-layouts  18.8 us (13%)
    pallas_call x1, Pallas kernels, exchange(): pl.pallas_call(exchange_kernel, out_shape=(jax.ShapeDtypeStruct((COLS, GA...  65 us
    pallas_call x1, Pallas kernels, spectrum(): pl.pallas_call(spectrum_kernel, out_shape=jax.ShapeDtypeStruct((16, NGV),...  33.8 us
    pallas_call x1, Pallas kernels, contract(): pl.pallas_call(response_kernel, out_shape=jax.ShapeDtypeStruct((2, GA, GB...  23.4 us
    unnamed x16, local copies, waits for them, and re-layouts  6.39 us
    gather x1, local copies, waits for them, and re-layouts, body(): c_rows = jnp.take(conduction, c, axis=1, mode='clip')  4.58 us
    gather x1, local copies, waits for them, and re-layouts, body(): v_rows = jnp.take(valence, v, axis=1, mode='clip')  3.53 us

profile of v1, /device:TPU:0, one launch (start us, length us, event | category | flops | bytes accessed | tf_op | source)
XLA Modules:
  0.0 141.2 jit_solution(2192652419910076998)
XLA Ops:
  0.0 0.0 copy-start
  0.0 0.8 slice_bitcast_fusion
  0.9 1.3 gather_fusion.3
  2.2 1.3 gather_fusion.2
  3.5 0.9 reshape.3.index_ref
  4.3 0.0 copy-done
  4.4 0.0 copy-start.5
  4.4 0.0 copy-start.7
  4.4 3.5 %gather_fusion = bf16[8,2,32768]{2,0,1:T(8,128)(2,1)S(1)} fusion(bf16[2,16,32768]{2,1,0:T(8,128)(2,1)S(1)} %copy-done, s32[1024]{0:T(1024)S(1)} %get-tuple-element.12), kind=kCustom, calls=%fused_computation | custom fusion | bytes 2097184 | tf_op jit(solution)/shard_map/jit(_take)/gather | solution.py:352
  7.9 4.6 %gather_fusion.1 = bf16[8,2,32768]{2,0,1:T(8,128)(2,1)} fusion(bf16[2,128,32768]{2,1,0:T(8,128)(2,1)} %param.11, s32[1024]{0:T(1024)S(1)} %get-tuple-element.11), kind=kCustom, calls=%fused_computation.1 | custom fusion | bytes 2097184 | tf_op jit(solution)/shard_map/jit(_take)/gather | solution.py:353
  12.5 0.0 copy-done.5
  12.5 0.0 copy-done.7
  12.5 0.0 copy-start.2
  12.5 1.2 copy-done.2
  13.7 0.0 copy-start.4
  13.7 1.2 copy-done.4
  15.0 0.0 copy-start.6
  15.0 0.9 copy-done.6
  15.9 33.8 %spectrum.1.y_ref = bf16[16,16384]{1,0:T(8,128)(2,1)S(1)} custom-call(bf16[2,8,32768]{2,1,0:T(8,128)(2,1)S(1)} %bitcast.6, bf16[2,8,32768]{2,1,0:T(8,128)(2,1)S(1)} %bitcast.7, f32[8]{0:T(128)S(1)} %sqrt_multiply_fusion.scale_ref, s32[32,512]{1,0:T(8,128)S(1)} %reshape.3.index_ref, bf16[2,512,512]{2,1,0:T(8,128)(2,1)S(1)} %copy-done.4, ...), custom_call_target="tpu_custom_call" | custom-call | tf_op jit(solution)/shard_map/spectrum/pallas_call | solution.py:112
  49.7 0.0 copy-start.3
  49.7 0.8 copy-done.3
  50.5 65.0 %exchange.1 = (bf16[16,2048,128]{2,1,0:T(8,128)(2,1)}, bf16[8,16,16,1024]{3,2,1,0:T(8,128)(2,1)}) custom-call(bf16[16,16384]{1,0:T(8,128)(2,1)} %copy-done.3), custom_call_target="tpu_custom_call" | custom-call | tf_op jit(solution)/shard_map/exchange/pallas_call | solution.py:292
  115.6 0.0 copy-start.1
  115.6 2.2 %copy-done.1 = bf16[8,16,16,1024]{3,2,1,0:T(8,128)(2,1)S(1)} copy-done((bf16[8,16,16,1024]{3,2,1,0:T(8,128)(2,1)S(1)}, bf16[8,16,16,1024]{3,2,1,0:T(8,128)(2,1)}, u32[]{:S(2)}) %copy-start.1) | copy-done | bytes 4194328
  117.8 23.4 %contract.1 = f32[2,2048,1024]{2,1,0:T(8,128)} custom-call(bf16[16,2048,128]{2,1,0:T(8,128)(2,1)} %get-tuple-element.7.a_ref, bf16[8,16,16,1024]{3,2,1,0:T(8,128)(2,1)S(1)} %copy-done.1), custom_call_target="tpu_custom_call" | custom-call | tf_op jit(solution)/shard_map/contract/pallas_call | solution.py:335
  (2 shorter events, 0.0 us)
Async XLA Ops:
  0.0 4.3 %copy-start = (bf16[2,16,32768]{2,1,0:T(8,128)(2,1)S(1)}, bf16[2,16,32768]{2,1,0:T(8,128)(2,1)}, u32[]{:S(2)}) copy-start(bf16[2,16,32768]{2,1,0:T(8,128)(2,1)} %param.10) | copy-start | bytes 6291460
  4.4 8.1 %copy-start.5 = (f32[2,256,128]{2,1,0:T(8,128)S(1)}, f32[2,256,128]{2,1,0:T(8,128)}, u32[]{:S(2)}) copy-start(f32[2,256,128]{2,1,0:T(8,128)} %constant.17.clone.tw_ref) | copy-start | bytes 786436
  4.4 8.1 %copy-start.7 = (bf16[16,128]{1,0:T(8,128)(2,1)S(1)}, bf16[16,128]{1,0:T(8,128)(2,1)}, u32[]{:S(2)}) copy-start(bf16[16,128]{1,0:T(8,128)(2,1)} %constant.18.clone.fold_ref) | copy-start | bytes 12292
  12.5 1.2 copy-start.2
  13.7 1.2 copy-start.4
  15.0 0.9 copy-start.6
  49.7 0.8 copy-start.3
  115.6 2.2 %copy-start.1 = (bf16[8,16,16,1024]{3,2,1,0:T(8,128)(2,1)S(1)}, bf16[8,16,16,1024]{3,2,1,0:T(8,128)(2,1)}, u32[]{:S(2)}) copy-start(bf16[8,16,16,1024]{3,2,1,0:T(8,128)(2,1)} %get-tuple-element.8.b_ref) | copy-start | bytes 12582916

commit v2 on v1

v2 whole, which is shorter than its diff:
```python
import math
import numpy as np
import jax
import jax.numpy as jnp
import ml_dtypes
from jax import lax
from jax.sharding import PartitionSpec as P
from jax.experimental import pallas as pl
from jax.experimental.pallas import tpu as pltpu

N1 = N2 = N3 = 32
KA, KB = 256, 128
NGV = 16384
GW = 1024


def split_np(t):
    hi = t.astype(ml_dtypes.bfloat16)
    lo = (t - hi.astype(np.float64)).astype(ml_dtypes.bfloat16)
    return hi, lo


def dft_tables():
    a = np.arange(KA)
    r1, r2a = a // 8, a % 8
    ph = (np.outer(r1, r1) / 32.0 + np.outer(r2a, r2a) / 8.0) % 1.0
    c, s = np.cos(2 * np.pi * ph), np.sin(2 * np.pi * ph)
    ta = np.block([[c, s], [-s, c]])
    b = np.arange(KB)
    r2b, r3 = b // 32, b % 32
    ph = (np.outer(r2b, r2b) / 4.0 + np.outer(r3, r3) / 32.0) % 1.0
    c, s = np.cos(2 * np.pi * ph), np.sin(2 * np.pi * ph)
    tb = np.block([[c, s], [-s, c]])
    ph = np.outer(r2a, r2b) / 32.0
    tw = np.stack([np.cos(2 * np.pi * ph), np.sin(2 * np.pi * ph)]).astype(np.float32)
    ta_hi, ta_lo = split_np(ta)
    tb_hi, tb_lo = split_np(tb)
    fold = np.zeros((16, 128), ml_dtypes.bfloat16)
    for p in range(8):
        for ri in range(2):
            fold[ri * 8 + p, p * 16 + ri * 8 : p * 16 + ri * 8 + 8] = 1
    return np.stack([ta_hi, ta_lo]), np.stack([tb_hi, tb_lo]), tw, fold


def split(x):
    hi = x.astype(jnp.bfloat16)
    return hi, (x - hi.astype(jnp.float32)).astype(jnp.bfloat16)


def dot_f32(a, b, dims):
    return lax.dot_general(a, b, (dims, ((), ())), preferred_element_type=jnp.float32)


def spectrum_kernel(v_ref, c_ref, scale_ref, ta_ref, tb_ref, tw_ref, xt, rr, ri):
    def products(a, _):
        lanes = pl.ds(pl.multiple_of(a * 128, 128), 128)
        vr, vi = v_ref[0, :, lanes].astype(jnp.float32), v_ref[1, :, lanes].astype(jnp.float32)
        cr, ci = c_ref[0, :, lanes].astype(jnp.float32), c_ref[1, :, lanes].astype(jnp.float32)
        rows = pl.ds(pl.multiple_of(a * 8, 8), 8)
        rr[rows, :] = vr * cr + vi * ci
        ri[rows, :] = vr * ci - vi * cr
        return 0

    lax.fori_loop(0, KA, products, 0, unroll=8)

    nn = ((1,), (0,))
    nt = ((1,), (1,))
    for h in range(4):
        x = jnp.concatenate(
            [
                jnp.concatenate([r[pl.ds(2 * h + q, KA, stride=8), :] for q in range(2)], axis=1)
                for r in (rr, ri)
            ],
            axis=0,
        )
        xh, xl = split(x)
        z = dot_f32(ta_ref[0], xh, nn) + (dot_f32(ta_ref[0], xl, nn) + dot_f32(ta_ref[1], xh, nn))
        for q in range(2):
            p = 2 * h + q
            zr, zi = z[:KA, q * KB : (q + 1) * KB], z[KA:, q * KB : (q + 1) * KB]
            t = jnp.concatenate([zr * tw_ref[0] + zi * tw_ref[1], zi * tw_ref[0] - zr * tw_ref[1]], axis=1)
            th, tl = split(t)
            s = dot_f32(tb_ref[0], th, nt) + (dot_f32(tb_ref[0], tl, nt) + dot_f32(tb_ref[1], th, nt))
            xt[p] = (s * scale_ref[p]).astype(jnp.bfloat16)

def spectrum(v_rows, c_rows, scale):
    ta, tb, tw, _ = dft_tables()
    vm = pl.BlockSpec(memory_space=pltpu.VMEM)
    return pl.pallas_call(
        spectrum_kernel,
        out_shape=jax.ShapeDtypeStruct((8, 256, 256), jnp.bfloat16),
        in_specs=[vm, vm, pl.BlockSpec(memory_space=pltpu.SMEM)] + [vm] * 3,
        out_specs=vm,
        scratch_shapes=[pltpu.VMEM((8 * KA, 128), jnp.float32)] * 2,
        compiler_params=pltpu.CompilerParams(vmem_limit_bytes=32 << 20),
        name="spectrum",
    )(v_rows, c_rows, scale, jnp.asarray(ta), jnp.asarray(tb), jnp.asarray(tw))


MESH = pl.DeviceIdType.MESH
ROWS, COLS = 8, 16
GA, GB = NGV // ROWS, NGV // COLS
SUB, SW = 4, 512
HALF, PART = SW // 2, SW // 4
STEPS = 28


def exchange_kernel(
    xt, index_ref, fold_ref, a_ref, b_ref, ys, pa, at,
    a0s, a0r, b0s, b0r, a1s, a1r, b1s, b1r, own_a, own_b, own_t,
):
    row, col = lax.axis_index("row"), lax.axis_index("col")
    x, core = row // 2, row % 2
    py, pz = col // 4, col % 4

    def cell(dy, dz):
        return lax.rem(py + dy + 4, 4) * 4 + lax.rem(pz + dz + 4, 4)

    def line(dx, dc=0):
        return lax.rem(x + dx + 4, 4) * 2 + lax.rem(core + dc, 2)

    def remote(src, dst, send, recv, device):
        return pltpu.make_async_remote_copy(
            src_ref=src, dst_ref=dst, send_sem=send, recv_sem=recv,
            device_id=device, device_id_type=MESH,
        )

    barrier = pltpu.get_barrier_semaphore()
    for d in range(1, ROWS):
        pl.semaphore_signal(barrier, inc=1, device_id=(lax.rem(row + d, ROWS), col), device_id_type=MESH)
    for d in range(1, COLS):
        pl.semaphore_signal(barrier, inc=1, device_id=(row, lax.rem(col + d, COLS)), device_id_type=MESH)
    pl.semaphore_wait(barrier, ROWS + COLS - 2)


    def select(s, m):
        k = jnp.concatenate([index_ref[pl.ds((2 * m + e) * SUB + s, 1), :] for e in range(2)], axis=1)
        ka = (k >> 10) * 8 + ((k >> 5) & 7)
        kb = ((k >> 8) & 3) * 32 + (k & 31)
        hot = jnp.where(lax.broadcasted_iota(jnp.int32, (KA, GW), 0) == ka, 1.0, 0.0).astype(jnp.bfloat16)
        kb_hi = jnp.broadcast_to(kb >> 3, (8, GW))
        low = lax.broadcasted_iota(jnp.int32, (8, GW), 0) == (kb & 7)
        parts = []
        for p in range(8):
            r = jnp.dot(xt[p], hot, preferred_element_type=jnp.float32)
            for q in range(2):
                acc = r[q * KB : q * KB + 8]
                for j in range(1, 16):
                    acc = jnp.where(kb_hi == j, r[q * KB + j * 8 : q * KB + j * 8 + 8], acc)
                parts.append(jnp.where(low, acc, 0.0))
        part = jnp.concatenate(parts, axis=0).astype(jnp.bfloat16)
        y = jnp.dot(fold_ref[...], part, preferred_element_type=jnp.float32).astype(jnp.bfloat16)
        for e in range(2):
            ys[s, 2 * m + e] = y[:, e * SW : (e + 1) * SW]


    def a0(s, i):
        return remote(ys.at[s, i], pa.at[s, row], a0s.at[s, i], a0r.at[s, row], (i, col))

    def b0(s, i):
        j = 2 * i + s // 2
        return remote(ys.at[s, i], b_ref.at[row, s % 2, col], b0s.at[s, i], b0r.at[s % 2, col], (row, j))

    def keep_a(s):
        return pltpu.make_async_copy(ys.at[s, row], pa.at[s, row], own_a.at[s])

    def keep_b(s):
        return pltpu.make_async_copy(ys.at[s, col // 2], b_ref.at[row, s % 2, col], own_b.at[s % 2])

    def hand_out(s, m):
        for e in range(2):
            i = 2 * m + e

            @pl.when(i != row)
            def _():
                a0(s, i).start()

            @pl.when(i == row)
            def _():
                keep_a(s).start()

            @pl.when(2 * i + s // 2 != col)
            def _():
                b0(s, i).start()

            @pl.when(2 * i + s // 2 == col)
            def _():
                keep_b(s).start()


    def along(h, first, d):
        return (row, cell(d, 0) if (h == 0) == first else cell(0, d))

    def spot(h, u, d):
        return cell(u, d) if h == 0 else cell(d, u)

    def rows(s, h, part=None):
        if part is None:
            return pl.ds(pl.multiple_of(s * SW + h * HALF, HALF), HALF)
        return pl.ds(pl.multiple_of(s * SW + h * HALF + part * PART, PART), PART)

    def a1(s, h, k, j, device, part=None, src=None):
        dst = a_ref.at[j, rows(s, h, part)]
        return remote(dst if src is None else src, dst, a1s.at[s, h, k], a1r.at[s, h, k], device)

    SIDES = ((0, 1), (1, -1))

    def second(s, h, slot, u):
        src = at.at[rows(s, h)] if u == 0 else None
        for n, d in SIDES:
            a1(s, h, 4 + slot * 4 + n, spot(h, u, 0), along(h, False, d), src=src).start()

    def keep_t(s):
        span = pl.ds(pl.multiple_of(s * SW, SW), SW)
        return pltpu.make_async_copy(at.at[span], a_ref.at[col, span], own_t.at[s])

    def turn(s):
        keep_a(s).wait()
        for d in range(1, ROWS):
            src = lax.rem(row + d, ROWS)
            remote(ys.at[s, row], pa.at[s, src], a0s.at[s, src], a0r.at[s, src], (src, col)).wait_recv()
        for n in range(SW // 128):
            block = pa[s, :, :, n * 128 : (n + 1) * 128].reshape(128, 128)
            span = pl.ds(pl.multiple_of(s * SW + n * 128, 128), 128)
            at[span, :] = block.astype(jnp.float32).T.astype(jnp.bfloat16)
        for h in range(2):
            for n, d in SIDES:
                a1(s, h, n, col, along(h, True, d), src=at.at[rows(s, h)]).start()
        keep_t(s).start()
        for h in range(2):
            second(s, h, 0, 0)

    def near(s):
        for n, d in SIDES:
            for h in range(2):
                j = spot(h, -d, 0)
                a1(s, h, n, j, (row, col)).wait_recv()
                a1(s, h, 2 + n, j, along(h, True, d), part=n).start()
                second(s, h, 1 + n, -d)

    def far(s):
        for h in range(2):
            for n in range(2):
                a1(s, h, 2 + n, spot(h, 2, 0), (row, col), part=n).wait_recv()
            second(s, h, 3, 2)

    SLOTS = ((0, 0), (1, -1), (2, 1), (3, 2))

    def pass_on(s, slot, u):
        for n, d in SIDES:
            for h in range(2):
                j = spot(h, u, -d)
                k = 4 + slot * 4 + n
                a1(s, h, k, j, (row, col)).wait_recv()
                a1(s, h, k + 2, j, along(h, False, d), part=n).start()

    def last(s, _):
        for slot, u in SLOTS:
            for n in range(2):
                for h in range(2):
                    a1(s, h, 6 + slot * 4 + n, spot(h, u, 2), (row, col), part=n).wait_recv()
        return 0


    def b1(f, k, i, device, part=None):
        ref = b_ref.at[i, f] if part is None else b_ref.at[i, f, pl.ds(part * 8, 8)]
        return remote(ref, ref, b1s.at[f, k], b1r.at[f, k], device)

    def sides(f):
        s = (col % 2) * 2 + f
        keep_b(s).wait()
        for d in range(1, COLS):
            src = lax.rem(col + d, COLS)
            remote(ys.at[s, 0], b_ref.at[row, f, src], b0s.at[s, 0], b0r.at[f, src], (row, src)).wait_recv()
        for n, d in SIDES:
            b1(f, n, row, (line(d), col)).start()
        b1(f, 2, row, (line(0, 1), col)).start()

    def sides_near(f):
        for n, d in SIDES:
            i = line(-d)
            b1(f, n, i, (row, col)).wait_recv()
            b1(f, 3 + n, i, (line(d), col), part=n).start()
            b1(f, 5 + n, i, (line(0, 1), col)).start()

    def sides_far(f):
        for n in range(2):
            b1(f, 3 + n, line(2), (row, col), part=n).wait_recv()
            b1(f, 7 + n, line(2), (line(0, 1), col), part=n).start()

    def sides_last(f, _):
        b1(f, 2, line(0, 1), (row, col)).wait_recv()
        for n, d in SIDES:
            b1(f, 5 + n, line(-d, 1), (row, col)).wait_recv()
            b1(f, 7 + n, line(2, 1), (row, col), part=n).wait_recv()
        return 0

    def step(n, _):
        @pl.when(n < 4 * SUB)
        def _():
            select(n // 4, n % 4)
            hand_out(n // 4, n % 4)

        def event(delay, run):
            s = (n - delay) // 4

            @pl.when((n >= delay) & (n < delay + 4 * SUB) & ((n - delay) % 4 == 0))
            def _():
                run(s)

        def column_event(delay, run):
            s = (n - delay) // 4

            @pl.when((n >= delay) & (n < delay + 4 * SUB) & ((n - delay) % 4 == 0) & (s // 2 == col % 2))
            def _():
                run(s % 2)

        event(5, turn)
        event(7, near)
        event(9, far)
        event(8, lambda s: pass_on(s, 0, 0))
        event(10, lambda s: pass_on(s, 1, -1))
        event(11, lambda s: pass_on(s, 2, 1))
        event(12, lambda s: pass_on(s, 3, 2))
        column_event(6, sides)
        column_event(10, sides_near)
        column_event(13, sides_far)
        return 0

    lax.fori_loop(0, STEPS, step, 0)
    lax.fori_loop(0, SUB, last, 0)
    lax.fori_loop(0, 2, sides_last, 0)


    def sent(s, _):
        keep_t(s).wait()
        for i in range(ROWS):
            @pl.when(i != row)
            def _():
                a0(s, i).wait_send()

            @pl.when(2 * i + s // 2 != col)
            def _():
                b0(s, i).wait_send()

        for h in range(2):
            for k in (0, 1) + tuple(4 + t * 4 + n for t in range(4) for n in range(2)):
                a1(s, h, k, col, (row, col)).wait_send()
                a1(s, h, k + 2, col, (row, col), part=0).wait_send()
        return 0

    def column_sent(f, _):
        for k in (0, 1, 2, 5, 6):
            b1(f, k, row, (row, col)).wait_send()
        for k in (3, 4, 7, 8):
            b1(f, k, row, (row, col), part=0).wait_send()
        return 0

    lax.fori_loop(0, SUB, sent, 0)
    lax.fori_loop(0, 2, column_sent, 0)


def exchange(xt, index):
    anywhere, vm = pl.BlockSpec(memory_space=pl.ANY), pl.BlockSpec(memory_space=pltpu.VMEM)
    dma = pltpu.SemaphoreType.DMA
    return pl.pallas_call(
        exchange_kernel,
        out_shape=(
            jax.ShapeDtypeStruct((COLS, GA, 128), jnp.bfloat16),
            jax.ShapeDtypeStruct((ROWS, 2, COLS, 16, SW), jnp.bfloat16),
        ),
        in_specs=[vm, vm, vm],
        out_specs=(anywhere, anywhere),
        scratch_shapes=[
            pltpu.VMEM((SUB, ROWS, 16, SW), jnp.bfloat16),
            pltpu.VMEM((SUB, ROWS, 16, SW), jnp.bfloat16),
            pltpu.VMEM((GA, 128), jnp.bfloat16),
            dma((SUB, ROWS)), dma((SUB, ROWS)),
            dma((SUB, ROWS)), dma((2, COLS)),
            dma((SUB, 2, 20)), dma((SUB, 2, 20)),
            dma((2, 9)), dma((2, 9)),
            dma((SUB,)), dma((2,)), dma((SUB,)),
        ],
        compiler_params=pltpu.CompilerParams(
            collective_id=0, has_side_effects=True, vmem_limit_bytes=32 << 20
        ),
        name="exchange",
    )(xt, index.reshape(ROWS * SUB, SW), jnp.asarray(dft_tables()[3]))


TM = 256


def response_kernel(a_ref, b_ref, o_ref, rhs):
    @pl.when(pl.program_id(0) == 0)
    def _():
        def build(n, _):
            i, j = n // COLS, lax.rem(n, COLS)
            block = jnp.concatenate([b_ref[i, f, j] for f in range(2)], axis=1).astype(jnp.float32)
            re, im = block[:8], block[8:]
            rows = pl.ds(pl.multiple_of(j * 128 + i * 16, 16), 16)
            rhs[rows, :GB] = (-block).astype(jnp.bfloat16)
            rhs[rows, GB:] = jnp.concatenate([-im, re], axis=0).astype(jnp.bfloat16)
            return 0

        lax.fori_loop(0, ROWS * COLS, build, 0)

    lhs = jnp.concatenate([a_ref[j] for j in range(COLS)], axis=1)
    for q in range(2):
        o_ref[q] = jnp.dot(lhs, rhs[:, q * GB : (q + 1) * GB], preferred_element_type=jnp.float32)


def contract(a, b):
    return pl.pallas_call(
        response_kernel,
        out_shape=jax.ShapeDtypeStruct((2, GA, GB), jnp.float32),
        grid=(GA // TM,),
        in_specs=[
            pl.BlockSpec((COLS, TM, 128), lambda m: (0, m, 0)),
            pl.BlockSpec((ROWS, 2, COLS, 16, SW), lambda m: (0, 0, 0, 0, 0), pipeline_mode=pl.Buffered(1)),
        ],
        out_specs=pl.BlockSpec((2, TM, GB), lambda m: (0, m, 0)),
        scratch_shapes=[pltpu.VMEM((COLS * 128, 2 * GB), jnp.bfloat16)],
        compiler_params=pltpu.CompilerParams(vmem_limit_bytes=48 << 20),
        name="contract",
    )(a, b)


def body(valence, conduction, valence_energy, conduction_energy, band_pairs, grid_index):
    v, c = band_pairs[:, 0], band_pairs[:, 1]
    v_rows = jnp.take(valence, v, axis=1, mode="clip")
    c_rows = jnp.take(conduction, c, axis=1, mode="clip")
    gap = jnp.take(valence_energy, v, mode="clip") - jnp.take(conduction_energy, c, mode="clip")
    scale = jnp.sqrt(-2.0 / (math.sqrt(1024) * gap)) / math.sqrt(N1 * N2 * N3)
    a, b = exchange(spectrum(v_rows, c_rows, scale), grid_index)
    return contract(a, b)


def solution(mesh):
    return jax.shard_map(
        body,
        mesh=mesh,
        in_specs=(P(), P(), P(), P(), P(("row", "col"), None), P()),
        out_specs=P(None, "row", "col"),
        check_vma=False,
    )
```

time: 142 us -> 126 us (0.89)
  Pallas kernels: 122 us -> 105 us
    pallas_call x1, Pallas kernels: 33.8 us -> 7.08 us  [spectrum(): pl.pallas_call(spectrum_kernel, out_shape=jax.ShapeDtypeStruct((8, 256, 2...]
    pallas_call x1, Pallas kernels: 65 us -> 74.8 us  [exchange(): pl.pallas_call(exchange_kernel, out_shape=(jax.ShapeDtypeStruct((COLS, GA...]
    unnamed x16 -> x14, local copies, waits for them, and re-layouts: 6.39 us -> 6.64 us
where the time goes in v2:
time: 126 us; the launch traced here: 125 us
  Pallas kernels  105 us (83%)
  local copies, waits for them, and re-layouts  19.1 us (15%)
    pallas_call x1, Pallas kernels, exchange(): pl.pallas_call(exchange_kernel, out_shape=(jax.ShapeDtypeStruct((COLS, GA...  74.8 us
    pallas_call x1, Pallas kernels, contract(): pl.pallas_call(response_kernel, out_shape=jax.ShapeDtypeStruct((2, GA, GB...  23.6 us
    pallas_call x1, Pallas kernels, spectrum(): pl.pallas_call(spectrum_kernel, out_shape=jax.ShapeDtypeStruct((8, 256, 2...  7.08 us
    unnamed x14, local copies, waits for them, and re-layouts  6.64 us
    gather x1, local copies, waits for them, and re-layouts, body(): c_rows = jnp.take(conduction, c, axis=1, mode='clip')  4.58 us
    gather x1, local copies, waits for them, and re-layouts, body(): v_rows = jnp.take(valence, v, axis=1, mode='clip')  3.53 us

profile of v2, /device:TPU:0, one launch (start us, length us, event | category | flops | bytes accessed | tf_op | source)
XLA Modules:
  0.0 124.6 jit_solution(15790273082503755622)
XLA Ops:
  0.0 0.0 copy-start
  0.0 0.8 slice_bitcast_fusion
  0.9 1.3 %gather_fusion.3 = f32[8]{0:T(128)S(1)} fusion(f32[128]{0:T(128)} %param.13, s32[1024]{0:T(1024)S(1)} %get-tuple-element.11), kind=kCustom, calls=%fused_computation.3 | custom fusion | bytes 96 | tf_op jit(solution)/shard_map/jit(_take)/gather | solution.py:433
  2.2 1.3 %gather_fusion.2 = f32[8]{0:T(128)S(1)} fusion(f32[16]{0:T(128)} %param.12, s32[1024]{0:T(1024)S(1)} %get-tuple-element.12), kind=kCustom, calls=%fused_computation.2 | custom fusion | bytes 96 | tf_op jit(solution)/shard_map/jit(_take)/gather | solution.py:433
  3.5 0.9 reshape.3.index_ref
  4.3 0.0 copy-done
  4.4 0.0 copy-start.4
  4.4 3.5 %gather_fusion = bf16[8,2,32768]{2,0,1:T(8,128)(2,1)S(1)} fusion(bf16[2,16,32768]{2,1,0:T(8,128)(2,1)S(1)} %copy-done, s32[1024]{0:T(1024)S(1)} %get-tuple-element.12), kind=kCustom, calls=%fused_computation | custom fusion | bytes 2097184 | tf_op jit(solution)/shard_map/jit(_take)/gather | solution.py:431
  7.9 0.0 copy-start.6
  7.9 4.6 %gather_fusion.1 = bf16[8,2,32768]{2,0,1:T(8,128)(2,1)} fusion(bf16[2,128,32768]{2,1,0:T(8,128)(2,1)} %param.11, s32[1024]{0:T(1024)S(1)} %get-tuple-element.11), kind=kCustom, calls=%fused_computation.1 | custom fusion | bytes 2097184 | tf_op jit(solution)/shard_map/jit(_take)/gather | solution.py:432
  12.5 0.0 copy-done.4
  12.5 0.0 copy-start.2
  12.5 1.2 copy-done.2
  13.7 0.0 copy-start.3
  13.7 1.2 copy-done.3
  14.9 0.0 copy-start.5
  15.0 0.9 copy-done.5
  15.9 7.1 %spectrum.1.xt = bf16[8,256,256]{2,1,0:T(8,128)(2,1)S(1)} custom-call(bf16[2,8,32768]{2,1,0:T(8,128)(2,1)S(1)} %bitcast.6, bf16[2,8,32768]{2,1,0:T(8,128)(2,1)S(1)} %bitcast.7, f32[8]{0:T(128)S(1)} %sqrt_multiply_fusion.scale_ref, bf16[2,512,512]{2,1,0:T(8,128)(2,1)S(1)} %copy-done.3, bf16[2,256,256]{2,1,0:T(8,128)(2,1)S(1)} %copy-done.5, ...), custom_call_target="tpu_custom_call" | custom-call | tf_op jit(solution)/shard_map/spectrum/pallas_call | solution.py:89
  23.0 0.0 copy-done.6
  23.0 74.8 %exchange.1 = (bf16[16,2048,128]{2,1,0:T(8,128)(2,1)S(1)}, bf16[8,2,16,16,512]{4,3,2,1,0:T(8,128)(2,1)S(1)}) custom-call(bf16[8,256,256]{2,1,0:T(8,128)(2,1)S(1)} %spectrum.1.xt, s32[32,512]{1,0:T(8,128)S(1)} %reshape.3.index_ref, bf16[16,128]{1,0:T(8,128)(2,1)S(1)} %copy-done.6), custom_call_target="tpu_custom_call" | custom-call | tf_op jit(solution)/shard_map/exchange/pallas_call | solution.py:366
  97.8 0.0 copy-start.1
  97.8 3.2 %copy-done.1 = bf16[16,2048,128]{2,1,0:T(8,128)(2,1)} copy-done((bf16[16,2048,128]{2,1,0:T(8,128)(2,1)}, bf16[16,2048,128]{2,1,0:T(8,128)(2,1)S(1)}, u32[]{:S(2)}) %copy-start.1) | copy-done | bytes 8388632
  101.0 23.6 %contract.1 = f32[2,2048,1024]{2,1,0:T(8,128)} custom-call(bf16[16,2048,128]{2,1,0:T(8,128)(2,1)} %copy-done.1, bf16[8,2,16,16,512]{4,3,2,1,0:T(8,128)(2,1)S(1)} %get-tuple-element.8.b_ref), custom_call_target="tpu_custom_call" | custom-call | tf_op jit(solution)/shard_map/contract/pallas_call | solution.py:414
  (2 shorter events, 0.0 us)
Async XLA Ops:
  0.0 4.3 %copy-start = (bf16[2,16,32768]{2,1,0:T(8,128)(2,1)S(1)}, bf16[2,16,32768]{2,1,0:T(8,128)(2,1)}, u32[]{:S(2)}) copy-start(bf16[2,16,32768]{2,1,0:T(8,128)(2,1)} %param.10) | copy-start | bytes 6291460
  4.4 8.1 %copy-start.4 = (f32[2,256,128]{2,1,0:T(8,128)S(1)}, f32[2,256,128]{2,1,0:T(8,128)}, u32[]{:S(2)}) copy-start(f32[2,256,128]{2,1,0:T(8,128)} %constant.17.clone.tw_ref) | copy-start | bytes 786436
  7.9 15.1 %copy-start.6 = (bf16[16,128]{1,0:T(8,128)(2,1)S(1)}, bf16[16,128]{1,0:T(8,128)(2,1)}, u32[]{:S(2)}) copy-start(bf16[16,128]{1,0:T(8,128)(2,1)} %constant.18.clone.fold_ref) | copy-start | bytes 12292
  12.5 1.2 copy-start.2
  13.7 1.2 copy-start.3
  14.9 0.9 copy-start.5
  97.8 3.2 %copy-start.1 = (bf16[16,2048,128]{2,1,0:T(8,128)(2,1)}, bf16[16,2048,128]{2,1,0:T(8,128)(2,1)S(1)}, u32[]{:S(2)}) copy-start(bf16[16,2048,128]{2,1,0:T(8,128)(2,1)S(1)} %get-tuple-element.7.a_ref) | copy-start | bytes 25165828

commit v3 on v2

--- a/solution.py
+++ b/solution.py
@@ -11,6 +11,7 @@
 N1 = N2 = N3 = 32
 KA, KB = 256, 128
 NGV = 16384
+NR = 32768
 GW = 1024
 
 
@@ -51,50 +52,101 @@
     return lax.dot_general(a, b, (dims, ((), ())), preferred_element_type=jnp.float32)
 
 
-def spectrum_kernel(v_ref, c_ref, scale_ref, ta_ref, tb_ref, tw_ref, xt, rr, ri):
-    def products(a, _):
+def spectrum_kernel(
+    bands, v_energy, c_energy, valence, conduction, ta_hbm, tb_hbm, tw_hbm, xt,
+    v_half, c_half, v_full, c_full, ta, tb, tw, sems,
+):
+    tables = [
+        pltpu.make_async_copy(src, dst, sems.at[k])
+        for k, (src, dst) in enumerate(((valence, v_half), (ta_hbm, ta), (tb_hbm, tb), (tw_hbm, tw)))
+    ]
+
+    def strip(p):
+        rows = pl.ds(pl.multiple_of(bands[p, 1] // 8 * 8, 8), 8)
+        return pltpu.make_async_copy(conduction.at[:, rows, :], c_half.at[p], sems.at[4 + p])
+
+    tables[0].start()
+    strip(0).start()
+    strip(1).start()
+    for copy in tables[1:]:
+        copy.start()
+    for p in range(2, 8):
+        strip(p).start()
+
+    tables[0].wait()
+
+    def widen_v(a, _):
         lanes = pl.ds(pl.multiple_of(a * 128, 128), 128)
-        vr, vi = v_ref[0, :, lanes].astype(jnp.float32), v_ref[1, :, lanes].astype(jnp.float32)
-        cr, ci = c_ref[0, :, lanes].astype(jnp.float32), c_ref[1, :, lanes].astype(jnp.float32)
-        rows = pl.ds(pl.multiple_of(a * 8, 8), 8)
-        rr[rows, :] = vr * cr + vi * ci
-        ri[rows, :] = vr * ci - vi * cr
-        return 0
-
-    lax.fori_loop(0, KA, products, 0, unroll=8)
+        rows = pl.ds(pl.multiple_of(a * 16, 16), 16)
+        for q in range(2):
+            v_full[q, rows, :] = v_half[q, :, lanes].astype(jnp.float32)
+        return 0
+
+    lax.fori_loop(0, KA, widen_v, 0, unroll=8)
 
     nn = ((1,), (0,))
     nt = ((1,), (1,))
     for h in range(4):
-        x = jnp.concatenate(
-            [
-                jnp.concatenate([r[pl.ds(2 * h + q, KA, stride=8), :] for q in range(2)], axis=1)
-                for r in (rr, ri)
-            ],
-            axis=0,
-        )
+        for e in range(2):
+            strip(2 * h + e).wait()
+
+        def widen_c(a, _):
+            lanes = pl.ds(pl.multiple_of(a * 128, 128), 128)
+            rows = pl.ds(pl.multiple_of(a * 8, 8), 8)
+            for e in range(2):
+                for q in range(2):
+                    c_full[h % 2, e, q, rows, :] = c_half[2 * h + e, q, :, lanes].astype(jnp.float32)
+            return 0
+
+        lax.fori_loop(0, KA, widen_c, 0, unroll=8)
+        real, imag = [], []
+        for e in range(2):
+            p = 2 * h + e
+            vr, vi = (v_full[q, pl.ds(bands[p, 0], KA, stride=16), :] for q in range(2))
+            cr, ci = (c_full[h % 2, e, q, pl.ds(bands[p, 1] % 8, KA, stride=8), :] for q in range(2))
+            real.append(vr * cr + vi * ci)
+            imag.append(vr * ci - vi * cr)
+        x = jnp.concatenate([jnp.concatenate(real, axis=1), jnp.concatenate(imag, axis=1)], axis=0)
+        if h == 0:
+            for copy in tables[1:]:
+                copy.wait()
         xh, xl = split(x)
-        z = dot_f32(ta_ref[0], xh, nn) + (dot_f32(ta_ref[0], xl, nn) + dot_f32(ta_ref[1], xh, nn))
-        for q in range(2):
-            p = 2 * h + q
-            zr, zi = z[:KA, q * KB : (q + 1) * KB], z[KA:, q * KB : (q + 1) * KB]
-            t = jnp.concatenate([zr * tw_ref[0] + zi * tw_ref[1], zi * tw_ref[0] - zr * tw_ref[1]], axis=1)
+        z = dot_f32(ta[0], xh, nn) + (dot_f32(ta[0], xl, nn) + dot_f32(ta[1], xh, nn))
+        for e in range(2):
+            p = 2 * h + e
+            zr, zi = z[:KA, e * KB : (e + 1) * KB], z[KA:, e * KB : (e + 1) * KB]
+            t = jnp.concatenate([zr * tw[0] + zi * tw[1], zi * tw[0] - zr * tw[1]], axis=1)
             th, tl = split(t)
-            s = dot_f32(tb_ref[0], th, nt) + (dot_f32(tb_ref[0], tl, nt) + dot_f32(tb_ref[1], th, nt))
-            xt[p] = (s * scale_ref[p]).astype(jnp.bfloat16)
-
-def spectrum(v_rows, c_rows, scale):
+            s = dot_f32(tb[0], th, nt) + (dot_f32(tb[0], tl, nt) + dot_f32(tb[1], th, nt))
+            gap = jnp.full((1, KA), v_energy[bands[p, 0]] - c_energy[bands[p, 1]], jnp.float32)
+            scale = jnp.sqrt(-2.0 / (math.sqrt(1024) * gap)) * (1.0 / math.sqrt(N1 * N2 * N3))
+            xt[p] = (s * scale).astype(jnp.bfloat16)
+
+
+def spectrum(valence, conduction, valence_energy, conduction_energy, band_pairs):
     ta, tb, tw, _ = dft_tables()
-    vm = pl.BlockSpec(memory_space=pltpu.VMEM)
+    anywhere = pl.BlockSpec(memory_space=pl.ANY)
+    scalars = pl.BlockSpec(memory_space=pltpu.SMEM)
+    bf, f32 = jnp.bfloat16, jnp.float32
     return pl.pallas_call(
         spectrum_kernel,
-        out_shape=jax.ShapeDtypeStruct((8, 256, 256), jnp.bfloat16),
-        in_specs=[vm, vm, pl.BlockSpec(memory_space=pltpu.SMEM)] + [vm] * 3,
-        out_specs=vm,
-        scratch_shapes=[pltpu.VMEM((8 * KA, 128), jnp.float32)] * 2,
-        compiler_params=pltpu.CompilerParams(vmem_limit_bytes=32 << 20),
+        out_shape=jax.ShapeDtypeStruct((8, 256, 256), bf),
+        in_specs=[scalars] * 3 + [anywhere] * 5,
+        out_specs=pl.BlockSpec(memory_space=pltpu.VMEM),
+        scratch_shapes=[
+            pltpu.VMEM((2, 16, NR), bf),
+            pltpu.VMEM((8, 2, 8, NR), bf),
+            pltpu.VMEM((2, KA * 16, 128), f32),
+            pltpu.VMEM((2, 2, 2, KA * 8, 128), f32),
+            pltpu.VMEM(ta.shape, bf),
+            pltpu.VMEM(tb.shape, bf),
+            pltpu.VMEM(tw.shape, f32),
+            pltpu.SemaphoreType.DMA((12,)),
+        ],
+        compiler_params=pltpu.CompilerParams(vmem_limit_bytes=48 << 20),
         name="spectrum",
-    )(v_rows, c_rows, scale, jnp.asarray(ta), jnp.asarray(tb), jnp.asarray(tw))
+    )(band_pairs, valence_energy, conduction_energy, valence, conduction,
+      jnp.asarray(ta), jnp.asarray(tb), jnp.asarray(tw))
 
 
 MESH = pl.DeviceIdType.MESH
@@ -427,12 +479,8 @@
 
 
 def body(valence, conduction, valence_energy, conduction_energy, band_pairs, grid_index):
-    v, c = band_pairs[:, 0], band_pairs[:, 1]
-    v_rows = jnp.take(valence, v, axis=1, mode="clip")
-    c_rows = jnp.take(conduction, c, axis=1, mode="clip")
-    gap = jnp.take(valence_energy, v, mode="clip") - jnp.take(conduction_energy, c, mode="clip")
-    scale = jnp.sqrt(-2.0 / (math.sqrt(1024) * gap)) / math.sqrt(N1 * N2 * N3)
-    a, b = exchange(spectrum(v_rows, c_rows, scale), grid_index)
+    xt = spectrum(valence, conduction, valence_energy, conduction_energy, band_pairs)
+    a, b = exchange(xt, grid_index)
     return contract(a, b)
 
 

time: 126 us -> 123 us (0.976)
  local copies, waits for them, and re-layouts: 19.1 us -> 10.9 us
  Pallas kernels: 105 us -> 111 us
    gather x4 -> x0, local copies, waits for them, and re-layouts: 10.7 us -> none  [the longest x1 4.58 us: body(): c_rows = jnp.take(conduction, c, axis=1, mode='clip')]
    pallas_call x1, Pallas kernels: 7.08 us -> 12.7 us  [spectrum(): pl.pallas_call(spectrum_kernel, out_shape=jax.ShapeDtypeStruct((8, 256, 2...]
    unnamed x14 -> x17, local copies, waits for them, and re-layouts: 6.64 us -> 10 us
where the time goes in v3:
time: 123 us; the launch traced here: 122 us
  Pallas kernels  111 us (90%)
  local copies, waits for them, and re-layouts  10.9 us (9%)
    pallas_call x1, Pallas kernels, exchange(): pl.pallas_call(exchange_kernel, out_shape=(jax.ShapeDtypeStruct((COLS, GA...  74.8 us
    pallas_call x1, Pallas kernels, contract(): pl.pallas_call(response_kernel, out_shape=jax.ShapeDtypeStruct((2, GA, GB...  23.6 us
    pallas_call x1, Pallas kernels, spectrum(): pl.pallas_call(spectrum_kernel, out_shape=jax.ShapeDtypeStruct((8, 256, 2...  12.7 us
    unnamed x17, local copies, waits for them, and re-layouts  10 us

profile of v3, /device:TPU:0, one launch (start us, length us, event | category | flops | bytes accessed | tf_op | source)
XLA Modules:
  0.0 122.0 jit_solution(414026228144863012)
XLA Ops:
  0.0 0.8 copy.11.bands
  0.8 0.9 reshape.3.index_ref
  1.6 0.0 copy-start.1
  1.6 1.6 %copy-done.1 = bf16[2,16,32768]{2,1,0:T(8,128)(2,1)S(1)} copy-done((bf16[2,16,32768]{2,1,0:T(8,128)(2,1)S(1)}, bf16[2,16,32768]{2,1,0:T(8,128)(2,1)}, u32[]{:S(2)}) %copy-start.1) | copy-done | bytes 2097176
  3.2 0.0 copy-start.2
  3.2 1.2 %copy-done.2 = bf16[2,512,512]{2,1,0:T(8,128)(2,1)S(1)} copy-done((bf16[2,512,512]{2,1,0:T(8,128)(2,1)S(1)}, bf16[2,512,512]{2,1,0:T(8,128)(2,1)}, u32[]{:S(2)}) %copy-start.2) | copy-done | bytes 1048600
  4.4 0.0 copy-start.3
  4.4 0.9 copy-done.3
  5.4 0.0 copy-start.4
  5.4 0.9 copy-done.4
  6.3 0.0 copy-start.6
  6.3 0.7 copy-done.6
  7.0 0.0 copy-start.7
  7.0 0.7 copy-done.7
  7.6 0.0 copy-start.5
  7.6 12.7 %spectrum.1.xt = bf16[8,256,256]{2,1,0:T(8,128)(2,1)S(1)} custom-call(s32[8,2]{1,0:T(8,128)S(1)} %copy.11.bands, f32[16]{0:T(128)S(1)} %copy-done.6, f32[128]{0:T(128)S(1)} %copy-done.7, bf16[2,16,32768]{2,1,0:T(8,128)(2,1)S(1)} %copy-done.1, bf16[2,128,32768]{2,1,0:T(8,128)(2,1)} %conduction.1, bf16[2,512,512]{2,1,0:T(8,128)(2,1)S(1)} %copy-done.2, ...), custom_call_target="tpu_custom_call" | custom-call | tf_op jit(solution)/shard_map/spectrum/pallas_call | solution.py:131
  20.3 0.0 copy-done.5
  20.4 74.8 %exchange.1 = (bf16[16,2048,128]{2,1,0:T(8,128)(2,1)S(1)}, bf16[8,2,16,16,512]{4,3,2,1,0:T(8,128)(2,1)S(1)}) custom-call(bf16[8,256,256]{2,1,0:T(8,128)(2,1)S(1)} %spectrum.1.xt, s32[32,512]{1,0:T(8,128)S(1)} %reshape.3.index_ref, bf16[16,128]{1,0:T(8,128)(2,1)S(1)} %copy-done.5), custom_call_target="tpu_custom_call" | custom-call | tf_op jit(solution)/shard_map/exchange/pallas_call | solution.py:418
  95.1 0.0 copy-start
  95.1 3.2 %copy-done = bf16[16,2048,128]{2,1,0:T(8,128)(2,1)} copy-done((bf16[16,2048,128]{2,1,0:T(8,128)(2,1)}, bf16[16,2048,128]{2,1,0:T(8,128)(2,1)S(1)}, u32[]{:S(2)}) %copy-start) | copy-done | bytes 8388632
  98.4 23.6 %contract.1 = f32[2,2048,1024]{2,1,0:T(8,128)} custom-call(bf16[16,2048,128]{2,1,0:T(8,128)(2,1)} %copy-done, bf16[8,2,16,16,512]{4,3,2,1,0:T(8,128)(2,1)S(1)} %get-tuple-element.8.b_ref), custom_call_target="tpu_custom_call" | custom-call | tf_op jit(solution)/shard_map/contract/pallas_call | solution.py:466
Async XLA Ops:
  1.6 1.6 %copy-start.1 = (bf16[2,16,32768]{2,1,0:T(8,128)(2,1)S(1)}, bf16[2,16,32768]{2,1,0:T(8,128)(2,1)}, u32[]{:S(2)}) copy-start(bf16[2,16,32768]{2,1,0:T(8,128)(2,1)} %valence.1) | copy-start | bytes 6291460
  3.2 1.2 %copy-start.2 = (bf16[2,512,512]{2,1,0:T(8,128)(2,1)S(1)}, bf16[2,512,512]{2,1,0:T(8,128)(2,1)}, u32[]{:S(2)}) copy-start(bf16[2,512,512]{2,1,0:T(8,128)(2,1)} %constant.8.clone.ta_hbm) | copy-start | bytes 3145732
  4.4 0.9 copy-start.3
  5.4 0.9 copy-start.4
  6.3 0.7 copy-start.6
  7.0 0.7 copy-start.7
  7.6 12.7 %copy-start.5 = (bf16[16,128]{1,0:T(8,128)(2,1)S(1)}, bf16[16,128]{1,0:T(8,128)(2,1)}, u32[]{:S(2)}) copy-start(bf16[16,128]{1,0:T(8,128)(2,1)} %constant.11.clone.fold_ref) | copy-start | bytes 12292
  95.1 3.2 %copy-start = (bf16[16,2048,128]{2,1,0:T(8,128)(2,1)}, bf16[16,2048,128]{2,1,0:T(8,128)(2,1)S(1)}, u32[]{:S(2)}) copy-start(bf16[16,2048,128]{2,1,0:T(8,128)(2,1)S(1)} %get-tuple-element.7.a_ref) | copy-start | bytes 25165828

commit v4 on v3

--- a/solution.py
+++ b/solution.py
@@ -125,7 +125,7 @@
 
 def spectrum(valence, conduction, valence_energy, conduction_energy, band_pairs):
     ta, tb, tw, _ = dft_tables()
-    anywhere = pl.BlockSpec(memory_space=pl.ANY)
+    anywhere = pl.BlockSpec(memory_space=pltpu.HBM)
     scalars = pl.BlockSpec(memory_space=pltpu.SMEM)
     bf, f32 = jnp.bfloat16, jnp.float32
     return pl.pallas_call(
@@ -154,22 +154,24 @@
 GA, GB = NGV // ROWS, NGV // COLS
 SUB, SW = 4, 512
 HALF, PART = SW // 2, SW // 4
-STEPS = 28
+SIDES = ((0, 1), (1, 3))
+SLOTS = (0, 3, 1, 2)
 
 
 def exchange_kernel(
     xt, index_ref, fold_ref, a_ref, b_ref, ys, pa, at,
-    a0s, a0r, b0s, b0r, a1s, a1r, b1s, b1r, own_a, own_b, own_t,
+    a0s, a0r, b0s, b0t, b0r, a1s, a1r, a1f, b1s, b1r, b1f, own_t,
 ):
     row, col = lax.axis_index("row"), lax.axis_index("col")
     x, core = row // 2, row % 2
-    py, pz = col // 4, col % 4
-
-    def cell(dy, dz):
-        return lax.rem(py + dy + 4, 4) * 4 + lax.rem(pz + dz + 4, 4)
-
-    def line(dx, dc=0):
-        return lax.rem(x + dx + 4, 4) * 2 + lax.rem(core + dc, 2)
+    ty, tz, tx = ([(v + d) % 4 for d in range(4)] for v in (col // 4, col % 4, x))
+    cell = [[ty[u] * 4 + tz[d] for d in range(4)] for u in range(4)]
+    line = [tx[d] * 2 + core for d in range(4)]
+    other = [tx[d] * 2 + 1 - core for d in range(4)]
+    to_row = [(row + d) % ROWS for d in range(ROWS)]
+    to_pair = [(col // 2 + d) % 8 for d in range(8)]
+    odd = col % 2
+    me = (row, col)
 
     def remote(src, dst, send, recv, device):
         return pltpu.make_async_remote_copy(
@@ -179,10 +181,9 @@
 
     barrier = pltpu.get_barrier_semaphore()
     for d in range(1, ROWS):
-        pl.semaphore_signal(barrier, inc=1, device_id=(lax.rem(row + d, ROWS), col), device_id_type=MESH)
+        pl.semaphore_signal(barrier, inc=1, device_id=(to_row[d], col), device_id_type=MESH)
     for d in range(1, COLS):
-        pl.semaphore_signal(barrier, inc=1, device_id=(row, lax.rem(col + d, COLS)), device_id_type=MESH)
-    pl.semaphore_wait(barrier, ROWS + COLS - 2)
+        pl.semaphore_signal(barrier, inc=1, device_id=(row, (col + d) % COLS), device_id_type=MESH)
 
 
     def select(s, m):
@@ -206,214 +207,177 @@
             ys[s, 2 * m + e] = y[:, e * SW : (e + 1) * SW]
 
 
-    def a0(s, i):
-        return remote(ys.at[s, i], pa.at[s, row], a0s.at[s, i], a0r.at[s, row], (i, col))
-
-    def b0(s, i):
-        j = 2 * i + s // 2
-        return remote(ys.at[s, i], b_ref.at[row, s % 2, col], b0s.at[s, i], b0r.at[s % 2, col], (row, j))
-
-    def keep_a(s):
-        return pltpu.make_async_copy(ys.at[s, row], pa.at[s, row], own_a.at[s])
-
-    def keep_b(s):
-        return pltpu.make_async_copy(ys.at[s, col // 2], b_ref.at[row, s % 2, col], own_b.at[s % 2])
-
-    def hand_out(s, m):
-        for e in range(2):
-            i = 2 * m + e
-
-            @pl.when(i != row)
-            def _():
-                a0(s, i).start()
-
-            @pl.when(i == row)
-            def _():
-                keep_a(s).start()
-
-            @pl.when(2 * i + s // 2 != col)
-            def _():
-                b0(s, i).start()
-
-            @pl.when(2 * i + s // 2 == col)
-            def _():
-                keep_b(s).start()
+    def b0(s, d, sem):
+        i = to_pair[d]
+        return remote(ys.at[s, i], b_ref.at[row, s % 2, col], sem, b0r.at[s % 2], (row, 2 * i + s // 2))
+
+    def hand_out(s):
+        if s == 0:
+            pl.semaphore_wait(barrier, ROWS + COLS - 2)
+        for d in range(1, ROWS):
+            i = to_row[d]
+            remote(ys.at[s, i], pa.at[s, row], a0s.at[s], a0r.at[s], (i, col)).start()
+        pltpu.make_async_copy(ys.at[s, row], pa.at[s, row], a0r.at[s]).start()
+        for d in range(1, 8):
+            b0(s, d, b0s.at[s]).start()
+
+        @pl.when(odd == s // 2)
+        def _():
+            pltpu.make_async_copy(ys.at[s, to_pair[0]], b_ref.at[row, s % 2, col], b0r.at[s % 2]).start()
+
+        @pl.when(odd != s // 2)
+        def _():
+            b0(s, 0, b0t.at[s]).start()
 
 
     def along(h, first, d):
-        return (row, cell(d, 0) if (h == 0) == first else cell(0, d))
+        return (row, cell[d][0] if (h == 0) == first else cell[0][d])
 
     def spot(h, u, d):
-        return cell(u, d) if h == 0 else cell(d, u)
+        return cell[u][d] if h == 0 else cell[d][u]
 
     def rows(s, h, part=None):
         if part is None:
-            return pl.ds(pl.multiple_of(s * SW + h * HALF, HALF), HALF)
-        return pl.ds(pl.multiple_of(s * SW + h * HALF + part * PART, PART), PART)
+            return pl.ds(s * SW + h * HALF, HALF)
+        return pl.ds(s * SW + h * HALF + part * PART, PART)
 
     def a1(s, h, k, j, device, part=None, src=None):
         dst = a_ref.at[j, rows(s, h, part)]
-        return remote(dst if src is None else src, dst, a1s.at[s, h, k], a1r.at[s, h, k], device)
-
-    SIDES = ((0, 1), (1, -1))
-
-    def second(s, h, slot, u):
+        recv = a1f.at[s] if k is None else a1r.at[s, h, k]
+        return remote(dst if src is None else src, dst, a1s.at[s], recv, device)
+
+    def second(s, h, slot):
+        u = SLOTS[slot]
         src = at.at[rows(s, h)] if u == 0 else None
         for n, d in SIDES:
-            a1(s, h, 4 + slot * 4 + n, spot(h, u, 0), along(h, False, d), src=src).start()
+            a1(s, h, 4 + slot * 2 + n, spot(h, u, 0), along(h, False, d), src=src).start()
 
     def keep_t(s):
-        span = pl.ds(pl.multiple_of(s * SW, SW), SW)
+        span = pl.ds(s * SW, SW)
         return pltpu.make_async_copy(at.at[span], a_ref.at[col, span], own_t.at[s])
 
     def turn(s):
-        keep_a(s).wait()
-        for d in range(1, ROWS):
-            src = lax.rem(row + d, ROWS)
-            remote(ys.at[s, row], pa.at[s, src], a0s.at[s, src], a0r.at[s, src], (src, col)).wait_recv()
+        remote(pa.at[s], pa.at[s], a0s.at[s], a0r.at[s], me).wait_recv()
         for n in range(SW // 128):
             block = pa[s, :, :, n * 128 : (n + 1) * 128].reshape(128, 128)
-            span = pl.ds(pl.multiple_of(s * SW + n * 128, 128), 128)
-            at[span, :] = block.astype(jnp.float32).T.astype(jnp.bfloat16)
+            at[s * SW + n * 128 : s * SW + (n + 1) * 128, :] = block.astype(jnp.float32).T.astype(jnp.bfloat16)
         for h in range(2):
             for n, d in SIDES:
                 a1(s, h, n, col, along(h, True, d), src=at.at[rows(s, h)]).start()
+        for h in range(2):
+            second(s, h, 0)
         keep_t(s).start()
-        for h in range(2):
-            second(s, h, 0, 0)
 
     def near(s):
         for n, d in SIDES:
             for h in range(2):
-                j = spot(h, -d, 0)
-                a1(s, h, n, j, (row, col)).wait_recv()
+                j = spot(h, 4 - d, 0)
+                a1(s, h, n, j, me).wait_recv()
                 a1(s, h, 2 + n, j, along(h, True, d), part=n).start()
-                second(s, h, 1 + n, -d)
+                second(s, h, 1 + n)
 
     def far(s):
         for h in range(2):
             for n in range(2):
-                a1(s, h, 2 + n, spot(h, 2, 0), (row, col), part=n).wait_recv()
-            second(s, h, 3, 2)
-
-    SLOTS = ((0, 0), (1, -1), (2, 1), (3, 2))
-
-    def pass_on(s, slot, u):
+                a1(s, h, 2 + n, spot(h, 2, 0), me, part=n).wait_recv()
+            second(s, h, 3)
+
+    def pass_on(s, slot):
+        u = SLOTS[slot]
         for n, d in SIDES:
             for h in range(2):
-                j = spot(h, u, -d)
-                k = 4 + slot * 4 + n
-                a1(s, h, k, j, (row, col)).wait_recv()
-                a1(s, h, k + 2, j, along(h, False, d), part=n).start()
-
-    def last(s, _):
-        for slot, u in SLOTS:
-            for n in range(2):
-                for h in range(2):
-                    a1(s, h, 6 + slot * 4 + n, spot(h, u, 2), (row, col), part=n).wait_recv()
-        return 0
+                j = spot(h, u, 4 - d)
+                a1(s, h, 4 + slot * 2 + n, j, me).wait_recv()
+                a1(s, h, None, j, along(h, False, d), part=n).start()
 
 
     def b1(f, k, i, device, part=None):
         ref = b_ref.at[i, f] if part is None else b_ref.at[i, f, pl.ds(part * 8, 8)]
-        return remote(ref, ref, b1s.at[f, k], b1r.at[f, k], device)
+        return remote(ref, ref, b1s.at[f], b1f.at[f] if k is None else b1r.at[f, k], device)
 
     def sides(f):
-        s = (col % 2) * 2 + f
-        keep_b(s).wait()
-        for d in range(1, COLS):
-            src = lax.rem(col + d, COLS)
-            remote(ys.at[s, 0], b_ref.at[row, f, src], b0s.at[s, 0], b0r.at[f, src], (row, src)).wait_recv()
+        ref = b_ref.at[row, f]
+        remote(ref, ref, b1s.at[f], b0r.at[f], me).wait_recv()
         for n, d in SIDES:
-            b1(f, n, row, (line(d), col)).start()
-        b1(f, 2, row, (line(0, 1), col)).start()
+            b1(f, n, row, (line[d], col)).start()
+        b1(f, None, row, (other[0], col)).start()
 
     def sides_near(f):
         for n, d in SIDES:
-            i = line(-d)
-            b1(f, n, i, (row, col)).wait_recv()
-            b1(f, 3 + n, i, (line(d), col), part=n).start()
-            b1(f, 5 + n, i, (line(0, 1), col)).start()
+            i = line[4 - d]
+            b1(f, n, i, me).wait_recv()
+            b1(f, 2 + n, i, (line[d], col), part=n).start()
+            b1(f, None, i, (other[0], col)).start()
 
     def sides_far(f):
         for n in range(2):
-            b1(f, 3 + n, line(2), (row, col), part=n).wait_recv()
-            b1(f, 7 + n, line(2), (line(0, 1), col), part=n).start()
-
-    def sides_last(f, _):
-        b1(f, 2, line(0, 1), (row, col)).wait_recv()
-        for n, d in SIDES:
-            b1(f, 5 + n, line(-d, 1), (row, col)).wait_recv()
-            b1(f, 7 + n, line(2, 1), (row, col), part=n).wait_recv()
+            b1(f, 2 + n, line[2], me, part=n).wait_recv()
+            b1(f, None, line[2], (other[0], col), part=n).start()
+
+
+    events = []
+    for s in range(SUB):
+        events.append((4 * s + 3.9, lambda s=s: hand_out(s)))
+        events.append((4 * s + TURN, lambda s=s: turn(s)))
+        events.append((4 * s + NEAR, lambda s=s: near(s)))
+        events.append((4 * s + FAR, lambda s=s: far(s)))
+        for slot in range(4):
+            events.append((PASS + PACE * s + 1.5 * slot, lambda s=s, slot=slot: pass_on(s, slot)))
+        for delay, run in ((7.1, sides), (12.1, sides_near), (16.1, sides_far)):
+            def guarded(s=s, run=run):
+                @pl.when(odd == s // 2)
+                def _():
+                    run(s % 2)
+
+            events.append((4 * s + delay, guarded))
+    events.sort(key=lambda e: e[0])
+
+    def step(n, _):
+        for e in range(2):
+            select(n // 2, (n % 2) * 2 + e)
+        for k in range(8):
+            now = [run for time, run in events if 2 * k <= time - 1.5 < 2 * k + 2]
+            if now:
+                @pl.when(n == k)
+                def _(now=now):
+                    for run in now:
+                        run()
         return 0
 
-    def step(n, _):
-        @pl.when(n < 4 * SUB)
+    lax.fori_loop(0, 8, step, 0)
+    for time, run in events:
+        if time - 1.5 >= 16:
+            run()
+
+
+    for s in range(SUB):
+        whole = a_ref.at[0]
+        remote(whole, whole, a1s.at[s], a1f.at[s], me).wait_recv()
+    for f in range(2):
+        span = b_ref.at[pl.ds(0, 4), f]
+        remote(span, span, b1s.at[f], b1f.at[f], me).wait_recv()
+    for s in range(SUB):
+        keep_t(s).wait()
+        span = ys.at[s, pl.ds(0, 7)]
+        remote(span, span, a0s.at[s], a0r.at[s], me).wait_send()
+        remote(span, span, b0s.at[s], a0r.at[s], me).wait_send()
+
+        @pl.when(odd != s // 2)
         def _():
-            select(n // 4, n % 4)
-            hand_out(n // 4, n % 4)
-
-        def event(delay, run):
-            s = (n - delay) // 4
-
-            @pl.when((n >= delay) & (n < delay + 4 * SUB) & ((n - delay) % 4 == 0))
-            def _():
-                run(s)
-
-        def column_event(delay, run):
-            s = (n - delay) // 4
-
-            @pl.when((n >= delay) & (n < delay + 4 * SUB) & ((n - delay) % 4 == 0) & (s // 2 == col % 2))
-            def _():
-                run(s % 2)
-
-        event(5, turn)
-        event(7, near)
-        event(9, far)
-        event(8, lambda s: pass_on(s, 0, 0))
-        event(10, lambda s: pass_on(s, 1, -1))
-        event(11, lambda s: pass_on(s, 2, 1))
-        event(12, lambda s: pass_on(s, 3, 2))
-        column_event(6, sides)
-        column_event(10, sides_near)
-        column_event(13, sides_far)
-        return 0
-
-    lax.fori_loop(0, STEPS, step, 0)
-    lax.fori_loop(0, SUB, last, 0)
-    lax.fori_loop(0, 2, sides_last, 0)
-
-
-    def sent(s, _):
-        keep_t(s).wait()
-        for i in range(ROWS):
-            @pl.when(i != row)
-            def _():
-                a0(s, i).wait_send()
-
-            @pl.when(2 * i + s // 2 != col)
-            def _():
-                b0(s, i).wait_send()
-
-        for h in range(2):
-            for k in (0, 1) + tuple(4 + t * 4 + n for t in range(4) for n in range(2)):
-                a1(s, h, k, col, (row, col)).wait_send()
-                a1(s, h, k + 2, col, (row, col), part=0).wait_send()
-        return 0
-
-    def column_sent(f, _):
-        for k in (0, 1, 2, 5, 6):
-            b1(f, k, row, (row, col)).wait_send()
-        for k in (3, 4, 7, 8):
-            b1(f, k, row, (row, col), part=0).wait_send()
-        return 0
-
-    lax.fori_loop(0, SUB, sent, 0)
-    lax.fori_loop(0, 2, column_sent, 0)
+            b0(s, 0, b0t.at[s]).wait_send()
+
+        span = a_ref.at[pl.ds(0, 15), pl.ds(0, SW)]
+        remote(span, span, a1s.at[s], a1f.at[s], me).wait_send()
+    for f in range(2):
+        span = b_ref.at[pl.ds(0, 7), f]
+        remote(span, span, b1s.at[f], b1f.at[f], me).wait_send()
+
+
+TURN, NEAR, FAR, PASS, PACE = 6, 8, 10, 10, 6
 
 
 def exchange(xt, index):
-    anywhere, vm = pl.BlockSpec(memory_space=pl.ANY), pl.BlockSpec(memory_space=pltpu.VMEM)
+    hbm, vm = pl.BlockSpec(memory_space=pltpu.HBM), pl.BlockSpec(memory_space=pltpu.VMEM)
     dma = pltpu.SemaphoreType.DMA
     return pl.pallas_call(
         exchange_kernel,
@@ -422,16 +386,16 @@
             jax.ShapeDtypeStruct((ROWS, 2, COLS, 16, SW), jnp.bfloat16),
         ),
         in_specs=[vm, vm, vm],
-        out_specs=(anywhere, anywhere),
+        out_specs=(hbm, hbm),
         scratch_shapes=[
             pltpu.VMEM((SUB, ROWS, 16, SW), jnp.bfloat16),
             pltpu.VMEM((SUB, ROWS, 16, SW), jnp.bfloat16),
             pltpu.VMEM((GA, 128), jnp.bfloat16),
-            dma((SUB, ROWS)), dma((SUB, ROWS)),
-            dma((SUB, ROWS)), dma((2, COLS)),
-            dma((SUB, 2, 20)), dma((SUB, 2, 20)),
-            dma((2, 9)), dma((2, 9)),
-            dma((SUB,)), dma((2,)), dma((SUB,)),
+            dma((SUB,)), dma((SUB,)),
+            dma((SUB,)), dma((SUB,)), dma((2,)),
+            dma((SUB,)), dma((SUB, 2, 12)), dma((SUB,)),
+            dma((2,)), dma((2, 4)), dma((2,)),
+            dma((SUB,)),
         ],
         compiler_params=pltpu.CompilerParams(
             collective_id=0, has_side_effects=True, vmem_limit_bytes=32 << 20

time: 123 us -> 121 us (0.984)
  no operation moved by 1% of the time
where the time goes in v4:
time: 121 us
  Pallas kernels  110 us (91%)
  local copies, waits for them, and re-layouts  10.9 us (9%)
    pallas_call x1, Pallas kernels, exchange(): pl.pallas_call(exchange_kernel, out_shape=(jax.ShapeDtypeStruct((COLS, GA...  73.6 us
    pallas_call x1, Pallas kernels, contract(): pl.pallas_call(response_kernel, out_shape=jax.ShapeDtypeStruct((2, GA, GB...  23.6 us
    pallas_call x1, Pallas kernels, spectrum(): pl.pallas_call(spectrum_kernel, out_shape=jax.ShapeDtypeStruct((8, 256, 2...  12.7 us
    unnamed x17, local copies, waits for them, and re-layouts  10 us

profile of v4, /device:TPU:0, one launch (start us, length us, event | category | flops | bytes accessed | tf_op | source)
XLA Modules:
  0.0 120.9 jit_solution(11393542673242733037)
XLA Ops:
  0.0 0.8 copy.11.bands
  0.8 0.9 reshape.3.index_ref
  1.6 0.0 copy-start.1
  1.6 1.6 %copy-done.1 = bf16[2,16,32768]{2,1,0:T(8,128)(2,1)S(1)} copy-done((bf16[2,16,32768]{2,1,0:T(8,128)(2,1)S(1)}, bf16[2,16,32768]{2,1,0:T(8,128)(2,1)}, u32[]{:S(2)}) %copy-start.1) | copy-done | bytes 2097176
  3.2 0.0 copy-start.2
  3.2 1.2 %copy-done.2 = bf16[2,512,512]{2,1,0:T(8,128)(2,1)S(1)} copy-done((bf16[2,512,512]{2,1,0:T(8,128)(2,1)S(1)}, bf16[2,512,512]{2,1,0:T(8,128)(2,1)}, u32[]{:S(2)}) %copy-start.2) | copy-done | bytes 1048600
  4.4 0.0 copy-start.3
  4.4 0.9 copy-done.3
  5.4 0.0 copy-start.4
  5.4 0.9 copy-done.4
  6.3 0.0 copy-start.6
  6.3 0.7 copy-done.6
  7.0 0.0 copy-start.7
  7.0 0.7 copy-done.7
  7.6 0.0 copy-start.5
  7.6 12.7 %spectrum.1.xt = bf16[8,256,256]{2,1,0:T(8,128)(2,1)S(1)} custom-call(s32[8,2]{1,0:T(8,128)S(1)} %copy.11.bands, f32[16]{0:T(128)S(1)} %copy-done.6, f32[128]{0:T(128)S(1)} %copy-done.7, bf16[2,16,32768]{2,1,0:T(8,128)(2,1)S(1)} %copy-done.1, bf16[2,128,32768]{2,1,0:T(8,128)(2,1)} %conduction.1, bf16[2,512,512]{2,1,0:T(8,128)(2,1)S(1)} %copy-done.2, ...), custom_call_target="tpu_custom_call" | custom-call | tf_op jit(solution)/shard_map/spectrum/pallas_call | solution.py:131
  20.3 0.0 copy-done.5
  20.4 73.6 %exchange.1 = (bf16[16,2048,128]{2,1,0:T(8,128)(2,1)S(1)}, bf16[8,2,16,16,512]{4,3,2,1,0:T(8,128)(2,1)S(1)}) custom-call(bf16[8,256,256]{2,1,0:T(8,128)(2,1)S(1)} %spectrum.1.xt, s32[32,512]{1,0:T(8,128)S(1)} %reshape.3.index_ref, bf16[16,128]{1,0:T(8,128)(2,1)S(1)} %copy-done.5), custom_call_target="tpu_custom_call" | custom-call | tf_op jit(solution)/shard_map/exchange/pallas_call | solution.py:382
  94.0 0.0 copy-start
  94.0 3.2 %copy-done = bf16[16,2048,128]{2,1,0:T(8,128)(2,1)} copy-done((bf16[16,2048,128]{2,1,0:T(8,128)(2,1)}, bf16[16,2048,128]{2,1,0:T(8,128)(2,1)S(1)}, u32[]{:S(2)}) %copy-start) | copy-done | bytes 8388632
  97.2 23.6 %contract.1 = f32[2,2048,1024]{2,1,0:T(8,128)} custom-call(bf16[16,2048,128]{2,1,0:T(8,128)(2,1)} %copy-done, bf16[8,2,16,16,512]{4,3,2,1,0:T(8,128)(2,1)S(1)} %get-tuple-element.8.b_ref), custom_call_target="tpu_custom_call" | custom-call | tf_op jit(solution)/shard_map/contract/pallas_call | solution.py:430
Async XLA Ops:
  1.6 1.6 %copy-start.1 = (bf16[2,16,32768]{2,1,0:T(8,128)(2,1)S(1)}, bf16[2,16,32768]{2,1,0:T(8,128)(2,1)}, u32[]{:S(2)}) copy-start(bf16[2,16,32768]{2,1,0:T(8,128)(2,1)} %valence.1) | copy-start | bytes 6291460
  3.2 1.2 %copy-start.2 = (bf16[2,512,512]{2,1,0:T(8,128)(2,1)S(1)}, bf16[2,512,512]{2,1,0:T(8,128)(2,1)}, u32[]{:S(2)}) copy-start(bf16[2,512,512]{2,1,0:T(8,128)(2,1)} %constant.8.clone.ta_hbm) | copy-start | bytes 3145732
  4.4 0.9 copy-start.3
  5.4 0.9 copy-start.4
  6.3 0.7 copy-start.6
  7.0 0.7 copy-start.7
  7.6 12.7 %copy-start.5 = (bf16[16,128]{1,0:T(8,128)(2,1)S(1)}, bf16[16,128]{1,0:T(8,128)(2,1)}, u32[]{:S(2)}) copy-start(bf16[16,128]{1,0:T(8,128)(2,1)} %constant.11.clone.fold_ref) | copy-start | bytes 12292
  94.0 3.2 %copy-start = (bf16[16,2048,128]{2,1,0:T(8,128)(2,1)}, bf16[16,2048,128]{2,1,0:T(8,128)(2,1)S(1)}, u32[]{:S(2)}) copy-start(bf16[16,2048,128]{2,1,0:T(8,128)(2,1)S(1)} %get-tuple-element.7.a_ref) | copy-start | bytes 25165828

commit v5 on v4

--- a/solution.py
+++ b/solution.py
@@ -53,17 +53,19 @@
 
 
 def spectrum_kernel(
-    bands, v_energy, c_energy, valence, conduction, ta_hbm, tb_hbm, tw_hbm, xt,
-    v_half, c_half, v_full, c_full, ta, tb, tw, sems,
+    bands, v_hbm, c_hbm, valence, conduction, ta_hbm, tb_hbm, tw_hbm, xt,
+    v_energy, c_energy, v_half, c_half, v_full, c_full, ta, tb, tw, sems,
 ):
     tables = [
         pltpu.make_async_copy(src, dst, sems.at[k])
-        for k, (src, dst) in enumerate(((valence, v_half), (ta_hbm, ta), (tb_hbm, tb), (tw_hbm, tw)))
+        for k, (src, dst) in enumerate(
+            ((valence, v_half), (ta_hbm, ta), (tb_hbm, tb), (tw_hbm, tw), (v_hbm, v_energy), (c_hbm, c_energy))
+        )
     ]
 
     def strip(p):
-        rows = pl.ds(pl.multiple_of(bands[p, 1] // 8 * 8, 8), 8)
-        return pltpu.make_async_copy(conduction.at[:, rows, :], c_half.at[p], sems.at[4 + p])
+        rows = pl.ds(pl.multiple_of(bands[1, p] // 8 * 8, 8), 8)
+        return pltpu.make_async_copy(conduction.at[:, rows, :], c_half.at[p], sems.at[6 + p])
 
     tables[0].start()
     strip(0).start()
@@ -102,8 +104,8 @@
         real, imag = [], []
         for e in range(2):
             p = 2 * h + e
-            vr, vi = (v_full[q, pl.ds(bands[p, 0], KA, stride=16), :] for q in range(2))
-            cr, ci = (c_full[h % 2, e, q, pl.ds(bands[p, 1] % 8, KA, stride=8), :] for q in range(2))
+            vr, vi = (v_full[q, pl.ds(bands[0, p], KA, stride=16), :] for q in range(2))
+            cr, ci = (c_full[h % 2, e, q, pl.ds(bands[1, p] % 8, KA, stride=8), :] for q in range(2))
             real.append(vr * cr + vi * ci)
             imag.append(vr * ci - vi * cr)
         x = jnp.concatenate([jnp.concatenate(real, axis=1), jnp.concatenate(imag, axis=1)], axis=0)
@@ -118,7 +120,7 @@
             t = jnp.concatenate([zr * tw[0] + zi * tw[1], zi * tw[0] - zr * tw[1]], axis=1)
             th, tl = split(t)
             s = dot_f32(tb[0], th, nt) + (dot_f32(tb[0], tl, nt) + dot_f32(tb[1], th, nt))
-            gap = jnp.full((1, KA), v_energy[bands[p, 0]] - c_energy[bands[p, 1]], jnp.float32)
+            gap = jnp.full((1, KA), v_energy[bands[0, p]] - c_energy[bands[1, p]], jnp.float32)
             scale = jnp.sqrt(-2.0 / (math.sqrt(1024) * gap)) * (1.0 / math.sqrt(N1 * N2 * N3))
             xt[p] = (s * scale).astype(jnp.bfloat16)
 
@@ -131,9 +133,11 @@
     return pl.pallas_call(
         spectrum_kernel,
         out_shape=jax.ShapeDtypeStruct((8, 256, 256), bf),
-        in_specs=[scalars] * 3 + [anywhere] * 5,
+        in_specs=[scalars] + [anywhere] * 7,
         out_specs=pl.BlockSpec(memory_space=pltpu.VMEM),
         scratch_shapes=[
+            pltpu.SMEM(valence_energy.shape, f32),
+            pltpu.SMEM(conduction_energy.shape, f32),
             pltpu.VMEM((2, 16, NR), bf),
             pltpu.VMEM((8, 2, 8, NR), bf),
             pltpu.VMEM((2, KA * 16, 128), f32),
@@ -141,12 +145,13 @@
             pltpu.VMEM(ta.shape, bf),
             pltpu.VMEM(tb.shape, bf),
             pltpu.VMEM(tw.shape, f32),
-            pltpu.SemaphoreType.DMA((12,)),
+            pltpu.SemaphoreType.DMA((14,)),
         ],
         compiler_params=pltpu.CompilerParams(vmem_limit_bytes=48 << 20),
         name="spectrum",
-    )(band_pairs, valence_energy, conduction_energy, valence, conduction,
-      jnp.asarray(ta), jnp.asarray(tb), jnp.asarray(tw))
+    )(band_pairs.T,
+      *(pltpu.with_memory_space_constraint(t, pltpu.HBM)
+        for t in (valence_energy, conduction_energy, valence, conduction, jnp.asarray(ta), jnp.asarray(tb), jnp.asarray(tw))))
 
 
 MESH = pl.DeviceIdType.MESH
@@ -159,7 +164,7 @@
 
 
 def exchange_kernel(
-    xt, index_ref, fold_ref, a_ref, b_ref, ys, pa, at,
+    xt, index_ref, fold_ref, a_ref, rhs, part_ref, b_ref, ys, pa, at,
     a0s, a0r, b0s, b0t, b0r, a1s, a1r, a1f, b1s, b1r, b1f, own_t,
 ):
     row, col = lax.axis_index("row"), lax.axis_index("col")
@@ -185,9 +190,12 @@
     for d in range(1, COLS):
         pl.semaphore_signal(barrier, inc=1, device_id=(row, (col + d) % COLS), device_id_type=MESH)
 
+    def place(s):
+        return s % 2 * 2 + s // 2
+
 
     def select(s, m):
-        k = jnp.concatenate([index_ref[pl.ds((2 * m + e) * SUB + s, 1), :] for e in range(2)], axis=1)
+        k = jnp.concatenate([index_ref[pl.ds((2 * m + e) * SUB + place(s), 1), :] for e in range(2)], axis=1)
         ka = (k >> 10) * 8 + ((k >> 5) & 7)
         kb = ((k >> 8) & 3) * 32 + (k & 31)
         hot = jnp.where(lax.broadcasted_iota(jnp.int32, (KA, GW), 0) == ka, 1.0, 0.0).astype(jnp.bfloat16)
@@ -209,7 +217,7 @@
 
     def b0(s, d, sem):
         i = to_pair[d]
-        return remote(ys.at[s, i], b_ref.at[row, s % 2, col], sem, b0r.at[s % 2], (row, 2 * i + s // 2))
+        return remote(ys.at[s, i], b_ref.at[row, s // 2, col], sem, b0r.at[s // 2], (row, 2 * i + s % 2))
 
     def hand_out(s):
         if s == 0:
@@ -221,11 +229,11 @@
         for d in range(1, 8):
             b0(s, d, b0s.at[s]).start()
 
-        @pl.when(odd == s // 2)
+        @pl.when(odd == s % 2)
         def _():
-            pltpu.make_async_copy(ys.at[s, to_pair[0]], b_ref.at[row, s % 2, col], b0r.at[s % 2]).start()
-
-        @pl.when(odd != s // 2)
+            pltpu.make_async_copy(ys.at[s, to_pair[0]], b_ref.at[row, s // 2, col], b0r.at[s // 2]).start()
+
+        @pl.when(odd != s % 2)
         def _():
             b0(s, 0, b0t.at[s]).start()
 
@@ -238,8 +246,8 @@
 
     def rows(s, h, part=None):
         if part is None:
-            return pl.ds(s * SW + h * HALF, HALF)
-        return pl.ds(s * SW + h * HALF + part * PART, PART)
+            return pl.ds(place(s) * SW + h * HALF, HALF)
+        return pl.ds(place(s) * SW + h * HALF + part * PART, PART)
 
     def a1(s, h, k, j, device, part=None, src=None):
         dst = a_ref.at[j, rows(s, h, part)]
@@ -253,14 +261,15 @@
             a1(s, h, 4 + slot * 2 + n, spot(h, u, 0), along(h, False, d), src=src).start()
 
     def keep_t(s):
-        span = pl.ds(s * SW, SW)
+        span = pl.ds(place(s) * SW, SW)
         return pltpu.make_async_copy(at.at[span], a_ref.at[col, span], own_t.at[s])
 
     def turn(s):
         remote(pa.at[s], pa.at[s], a0s.at[s], a0r.at[s], me).wait_recv()
         for n in range(SW // 128):
             block = pa[s, :, :, n * 128 : (n + 1) * 128].reshape(128, 128)
-            at[s * SW + n * 128 : s * SW + (n + 1) * 128, :] = block.astype(jnp.float32).T.astype(jnp.bfloat16)
+            start = place(s) * SW + n * 128
+            at[start : start + 128, :] = block.astype(jnp.float32).T.astype(jnp.bfloat16)
         for h in range(2):
             for n, d in SIDES:
                 a1(s, h, n, col, along(h, True, d), src=at.at[rows(s, h)]).start()
@@ -323,11 +332,11 @@
         events.append((4 * s + FAR, lambda s=s: far(s)))
         for slot in range(4):
             events.append((PASS + PACE * s + 1.5 * slot, lambda s=s, slot=slot: pass_on(s, slot)))
-        for delay, run in ((7.1, sides), (12.1, sides_near), (16.1, sides_far)):
+        for delay, run in ((7.1, sides), (11.6, sides_near), (15.4, sides_far)):
             def guarded(s=s, run=run):
-                @pl.when(odd == s // 2)
+                @pl.when(odd == s % 2)
                 def _():
-                    run(s % 2)
+                    run(s // 2)
 
             events.append((4 * s + delay, guarded))
     events.sort(key=lambda e: e[0])
@@ -336,7 +345,7 @@
         for e in range(2):
             select(n // 2, (n % 2) * 2 + e)
         for k in range(8):
-            now = [run for time, run in events if 2 * k <= time - 1.5 < 2 * k + 2]
+            now = [run for time, run in events if 2 * k + 1.5 <= time < 2 * k + 3.5]
             if now:
                 @pl.when(n == k)
                 def _(now=now):
@@ -346,23 +355,70 @@
 
     lax.fori_loop(0, 8, step, 0)
     for time, run in events:
-        if time - 1.5 >= 16:
+        if 17.5 <= time < UNITS[0]:
             run()
 
 
-    for s in range(SUB):
+    def build(f):
+        span = b_ref.at[pl.ds(0, 4), f]
+        remote(span, span, b1s.at[f], b1f.at[f], me).wait_recv()
+
+        def cross(n, _):
+            i, j = n // COLS, n % COLS
+            block = b_ref[i, f, j].astype(jnp.float32)
+            span = pl.ds(pl.multiple_of(j * 128 + i * 16, 16), 16)
+            rhs[f, span, :SW] = (-block).astype(jnp.bfloat16)
+            rhs[f, span, SW:] = jnp.concatenate([-block[8:], block[:8]], axis=0).astype(jnp.bfloat16)
+            return 0
+
+        lax.fori_loop(0, ROWS * COLS, cross, 0, unroll=4)
+
+    def complete(s):
         whole = a_ref.at[0]
         remote(whole, whole, a1s.at[s], a1f.at[s], me).wait_recv()
-    for f in range(2):
-        span = b_ref.at[pl.ds(0, 4), f]
-        remote(span, span, b1s.at[f], b1f.at[f], me).wait_recv()
+        keep_t(s).wait()
+
+    ready = {0: [lambda: complete(0), lambda: build(0)], 1: [lambda: complete(1)], 2: [lambda: build(1)],
+             4: [lambda: complete(2)]}
+
+    def unit(t, _):
+        for k, runs in ready.items():
+            @pl.when(t == k)
+            def _(runs=runs):
+                for run in runs:
+                    run()
+
+        late = t // 4
+        f = (1 - late) * (t // 2) + late * (t % 2)
+        block = (1 - late) * (t % 2) * 2 + late
+        for e in range(SW // TM):
+            span = pl.ds(pl.multiple_of(block * SW + e * TM, TM), TM)
+            lhs = jnp.concatenate([a_ref[j, span, :] for j in range(COLS)], axis=1)
+            for q in range(2):
+                part_ref[q, f, span, :] = jnp.dot(
+                    lhs, rhs[f, :, q * SW : (q + 1) * SW], preferred_element_type=jnp.float32
+                )
+        for k in range(len(UNITS)):
+            upper = UNITS[k + 1] if k + 1 < len(UNITS) else 1e9
+            now = [run for time, run in events if UNITS[k] <= time < upper]
+            if now:
+                @pl.when(t == k)
+                def _(now=now):
+                    for run in now:
+                        run()
+        return 0
+
+    lax.fori_loop(0, len(UNITS), unit, 0)
+
+
+    for s in range(READY // SW, SUB):
+        complete(s)
     for s in range(SUB):
-        keep_t(s).wait()
         span = ys.at[s, pl.ds(0, 7)]
         remote(span, span, a0s.at[s], a0r.at[s], me).wait_send()
         remote(span, span, b0s.at[s], a0r.at[s], me).wait_send()
 
-        @pl.when(odd != s // 2)
+        @pl.when(odd != s % 2)
         def _():
             b0(s, 0, b0t.at[s]).wait_send()
 
@@ -374,20 +430,25 @@
 
 
 TURN, NEAR, FAR, PASS, PACE = 6, 8, 10, 10, 6
+UNITS = (21, 24, 31.1, 33, 34, 35)
+TM = 256
+READY = 1536
 
 
 def exchange(xt, index):
-    hbm, vm = pl.BlockSpec(memory_space=pltpu.HBM), pl.BlockSpec(memory_space=pltpu.VMEM)
+    vm = pl.BlockSpec(memory_space=pltpu.VMEM)
     dma = pltpu.SemaphoreType.DMA
     return pl.pallas_call(
         exchange_kernel,
         out_shape=(
             jax.ShapeDtypeStruct((COLS, GA, 128), jnp.bfloat16),
-            jax.ShapeDtypeStruct((ROWS, 2, COLS, 16, SW), jnp.bfloat16),
+            jax.ShapeDtypeStruct((2, COLS * 128, GB), jnp.bfloat16),
+            jax.ShapeDtypeStruct((2, 2, READY, SW), jnp.float32),
         ),
         in_specs=[vm, vm, vm],
-        out_specs=(hbm, hbm),
+        out_specs=(vm, vm, vm),
         scratch_shapes=[
+            pltpu.VMEM((ROWS, 2, COLS, 16, SW), jnp.bfloat16),
             pltpu.VMEM((SUB, ROWS, 16, SW), jnp.bfloat16),
             pltpu.VMEM((SUB, ROWS, 16, SW), jnp.bfloat16),
             pltpu.VMEM((GA, 128), jnp.bfloat16),
@@ -398,54 +459,59 @@
             dma((SUB,)),
         ],
         compiler_params=pltpu.CompilerParams(
-            collective_id=0, has_side_effects=True, vmem_limit_bytes=32 << 20
+            collective_id=0, has_side_effects=True, vmem_limit_bytes=24 << 20
         ),
         name="exchange",
     )(xt, index.reshape(ROWS * SUB, SW), jnp.asarray(dft_tables()[3]))
 
 
-TM = 256
-
-
-def response_kernel(a_ref, b_ref, o_ref, rhs):
-    @pl.when(pl.program_id(0) == 0)
-    def _():
-        def build(n, _):
-            i, j = n // COLS, lax.rem(n, COLS)
-            block = jnp.concatenate([b_ref[i, f, j] for f in range(2)], axis=1).astype(jnp.float32)
-            re, im = block[:8], block[8:]
-            rows = pl.ds(pl.multiple_of(j * 128 + i * 16, 16), 16)
-            rhs[rows, :GB] = (-block).astype(jnp.bfloat16)
-            rhs[rows, GB:] = jnp.concatenate([-im, re], axis=0).astype(jnp.bfloat16)
-            return 0
-
-        lax.fori_loop(0, ROWS * COLS, build, 0)
-
-    lhs = jnp.concatenate([a_ref[j] for j in range(COLS)], axis=1)
+TAIL = 128
+
+
+def response_kernel(a_ref, rhs, part_ref, o_ref, stage, sems):
+    copies = []
+
+    def out(src, q, f, rows):
+        copy = pltpu.make_async_copy(src, o_ref.at[q, rows, pl.ds(f * SW, SW)], sems.at[len(copies)])
+        copy.start()
+        copies.append(copy)
+
     for q in range(2):
-        o_ref[q] = jnp.dot(lhs, rhs[:, q * GB : (q + 1) * GB], preferred_element_type=jnp.float32)
-
-
-def contract(a, b):
+        for f in range(2):
+            out(part_ref.at[q, f], q, f, pl.ds(0, READY))
+    for t in range((GA - READY) // TAIL):
+        rows = pl.ds(READY + t * TAIL, TAIL)
+        lhs = jnp.concatenate([a_ref[j, rows, :] for j in range(COLS)], axis=1)
+        for f in range(2):
+            for q in range(2):
+                stage[t, q, f] = jnp.dot(
+                    lhs, rhs[f, :, q * SW : (q + 1) * SW], preferred_element_type=jnp.float32
+                )
+                out(stage.at[t, q, f], q, f, rows)
+    for copy in copies:
+        copy.wait()
+
+
+def contract(a, rhs, part):
+    vm = pl.BlockSpec(memory_space=pltpu.VMEM)
+    tiles = (GA - READY) // TAIL
     return pl.pallas_call(
         response_kernel,
         out_shape=jax.ShapeDtypeStruct((2, GA, GB), jnp.float32),
-        grid=(GA // TM,),
-        in_specs=[
-            pl.BlockSpec((COLS, TM, 128), lambda m: (0, m, 0)),
-            pl.BlockSpec((ROWS, 2, COLS, 16, SW), lambda m: (0, 0, 0, 0, 0), pipeline_mode=pl.Buffered(1)),
+        in_specs=[vm, vm, vm],
+        out_specs=pl.BlockSpec(memory_space=pltpu.HBM),
+        scratch_shapes=[
+            pltpu.VMEM((tiles, 2, 2, TAIL, SW), jnp.float32),
+            pltpu.SemaphoreType.DMA((4 + 4 * tiles,)),
         ],
-        out_specs=pl.BlockSpec((2, TM, GB), lambda m: (0, m, 0)),
-        scratch_shapes=[pltpu.VMEM((COLS * 128, 2 * GB), jnp.bfloat16)],
-        compiler_params=pltpu.CompilerParams(vmem_limit_bytes=48 << 20),
+        compiler_params=pltpu.CompilerParams(vmem_limit_bytes=24 << 20),
         name="contract",
-    )(a, b)
+    )(a, rhs, part)
 
 
 def body(valence, conduction, valence_energy, conduction_energy, band_pairs, grid_index):
     xt = spectrum(valence, conduction, valence_energy, conduction_energy, band_pairs)
-    a, b = exchange(xt, grid_index)
-    return contract(a, b)
+    return contract(*exchange(xt, grid_index))
 
 
 def solution(mesh):

time: 121 us -> 100 us (0.83)
  Pallas kernels: 110 us -> 98.2 us
  local copies, waits for them, and re-layouts: 10.9 us -> 1.54 us
    pallas_call x1, Pallas kernels: 23.6 us -> 6.05 us  [contract(): pl.pallas_call(response_kernel, out_shape=jax.ShapeDtypeStruct((2, GA, GB...]
    unnamed x17 -> x4, local copies, waits for them, and re-layouts: 10 us -> 0.68 us
    pallas_call x1, Pallas kernels: 73.6 us -> 79 us  [exchange(): pl.pallas_call(exchange_kernel, out_shape=(jax.ShapeDtypeStruct((COLS, GA...]
where the time goes in v5:
time: 100 us
  Pallas kernels  98.2 us (98%)
  local copies, waits for them, and re-layouts  1.54 us (2%)
    pallas_call x1, Pallas kernels, exchange(): pl.pallas_call(exchange_kernel, out_shape=(jax.ShapeDtypeStruct((COLS, GA...  79 us
    pallas_call x1, Pallas kernels, spectrum(): pl.pallas_call(spectrum_kernel, out_shape=jax.ShapeDtypeStruct((8, 256, 2...  13.2 us
    pallas_call x1, Pallas kernels, contract(): pl.pallas_call(response_kernel, out_shape=jax.ShapeDtypeStruct((2, GA, GB...  6.05 us

profile of v5, /device:TPU:0, one launch (start us, length us, event | category | flops | bytes accessed | tf_op | source)
XLA Modules:
  0.0 100.0 jit_solution(15154040970460357090)
XLA Ops:
  0.0 0.0 copy-start
  0.0 0.9 reshape.3.index_ref
  0.9 0.0 copy-start.1
  0.9 0.7 copy-done.1
  1.6 13.2 %spectrum.1.xt = bf16[8,256,256]{2,1,0:T(8,128)(2,1)S(1)} custom-call(s32[2,8]{1,0:T(2,128)S(1)} %bitcast.1, f32[16]{0:T(128)} %v_hbm.1, f32[128]{0:T(128)} %c_hbm.1, bf16[2,16,32768]{2,1,0:T(8,128)(2,1)} %valence.1, bf16[2,128,32768]{2,1,0:T(8,128)(2,1)} %conduction.1, bf16[2,512,512]{2,1,0:T(8,128)(2,1)} %constant.8.clone.ta_hbm, ...), custom_call_target="tpu_custom_call" | custom-call | tf_op jit(solution)/shard_map/spectrum/pallas_call | solution.py:133
  14.8 0.0 copy-done
  14.8 79.0 %exchange.1 = (bf16[16,2048,128]{2,1,0:T(8,128)(2,1)S(1)}, bf16[2,2048,1024]{2,1,0:T(8,128)(2,1)S(1)}, f32[2,2,1536,512]{3,2,1,0:T(8,128)S(1)}) custom-call(bf16[8,256,256]{2,1,0:T(8,128)(2,1)S(1)} %spectrum.1.xt, s32[32,512]{1,0:T(8,128)S(1)} %reshape.3.index_ref, bf16[16,128]{1,0:T(8,128)(2,1)S(1)} %copy-done), custom_call_target="tpu_custom_call" | custom-call | tf_op jit(solution)/shard_map/exchange/pallas_call | solution.py:441
  93.8 6.1 %contract.1 = f32[2,2048,1024]{2,1,0:T(8,128)} custom-call(bf16[16,2048,128]{2,1,0:T(8,128)(2,1)S(1)} %get-tuple-element.8.a_ref, bf16[2,2048,1024]{2,1,0:T(8,128)(2,1)S(1)} %get-tuple-element.9.rhs, f32[2,2,1536,512]{3,2,1,0:T(8,128)S(1)} %get-tuple-element.10.part_ref), custom_call_target="tpu_custom_call" | custom-call | tf_op jit(solution)/shard_map/contract/pallas_call | solution.py:498
Async XLA Ops:
  0.0 14.8 %copy-start = (bf16[16,128]{1,0:T(8,128)(2,1)S(1)}, bf16[16,128]{1,0:T(8,128)(2,1)}, u32[]{:S(2)}) copy-start(bf16[16,128]{1,0:T(8,128)(2,1)} %constant.11.clone.fold_ref) | copy-start | bytes 12292
  0.9 0.7 copy-start.1

commit v6 on v5

--- a/solution.py
+++ b/solution.py
@@ -12,7 +12,7 @@
 KA, KB = 256, 128
 NGV = 16384
 NR = 32768
-GW = 1024
+GW = 2048
 
 
 def split_np(t):
@@ -88,19 +88,21 @@
 
     nn = ((1,), (0,))
     nt = ((1,), (1,))
-    for h in range(4):
+
+    def widen_c(h):
         for e in range(2):
             strip(2 * h + e).wait()
-
-        def widen_c(a, _):
-            lanes = pl.ds(pl.multiple_of(a * 128, 128), 128)
-            rows = pl.ds(pl.multiple_of(a * 8, 8), 8)
+        for a in range(KA):
             for e in range(2):
                 for q in range(2):
-                    c_full[h % 2, e, q, rows, :] = c_half[2 * h + e, q, :, lanes].astype(jnp.float32)
-            return 0
-
-        lax.fori_loop(0, KA, widen_c, 0, unroll=8)
+                    c_full[h % 2, e, q, a * 8 : a * 8 + 8, :] = c_half[
+                        2 * h + e, q, :, a * 128 : a * 128 + 128
+                    ].astype(jnp.float32)
+
+    widen_c(0)
+    for copy in tables[1:]:
+        copy.wait()
+    for h in range(4):
         real, imag = [], []
         for e in range(2):
             p = 2 * h + e
@@ -109,17 +111,20 @@
             real.append(vr * cr + vi * ci)
             imag.append(vr * ci - vi * cr)
         x = jnp.concatenate([jnp.concatenate(real, axis=1), jnp.concatenate(imag, axis=1)], axis=0)
-        if h == 0:
-            for copy in tables[1:]:
-                copy.wait()
         xh, xl = split(x)
-        z = dot_f32(ta[0], xh, nn) + (dot_f32(ta[0], xl, nn) + dot_f32(ta[1], xh, nn))
+        z = dot_f32(
+            jnp.concatenate([ta[0], ta[0], ta[1]], axis=1), jnp.concatenate([xh, xl, xh], axis=0), nn
+        )
+        if h < 3:
+            widen_c(h + 1)
         for e in range(2):
             p = 2 * h + e
             zr, zi = z[:KA, e * KB : (e + 1) * KB], z[KA:, e * KB : (e + 1) * KB]
             t = jnp.concatenate([zr * tw[0] + zi * tw[1], zi * tw[0] - zr * tw[1]], axis=1)
             th, tl = split(t)
-            s = dot_f32(tb[0], th, nt) + (dot_f32(tb[0], tl, nt) + dot_f32(tb[1], th, nt))
+            s = dot_f32(
+                jnp.concatenate([tb[0], tb[0], tb[1]], axis=1), jnp.concatenate([th, tl, th], axis=1), nt
+            )
             gap = jnp.full((1, KA), v_energy[bands[0, p]] - c_energy[bands[1, p]], jnp.float32)
             scale = jnp.sqrt(-2.0 / (math.sqrt(1024) * gap)) * (1.0 / math.sqrt(N1 * N2 * N3))
             xt[p] = (s * scale).astype(jnp.bfloat16)
@@ -195,7 +200,7 @@
 
 
     def select(s, m):
-        k = jnp.concatenate([index_ref[pl.ds((2 * m + e) * SUB + place(s), 1), :] for e in range(2)], axis=1)
+        k = jnp.concatenate([index_ref[pl.ds((4 * m + e) * SUB + place(s), 1), :] for e in range(4)], axis=1)
         ka = (k >> 10) * 8 + ((k >> 5) & 7)
         kb = ((k >> 8) & 3) * 32 + (k & 31)
         hot = jnp.where(lax.broadcasted_iota(jnp.int32, (KA, GW), 0) == ka, 1.0, 0.0).astype(jnp.bfloat16)
@@ -211,8 +216,8 @@
                 parts.append(jnp.where(low, acc, 0.0))
         part = jnp.concatenate(parts, axis=0).astype(jnp.bfloat16)
         y = jnp.dot(fold_ref[...], part, preferred_element_type=jnp.float32).astype(jnp.bfloat16)
-        for e in range(2):
-            ys[s, 2 * m + e] = y[:, e * SW : (e + 1) * SW]
+        for e in range(4):
+            ys[s, 4 * m + e] = y[:, e * SW : (e + 1) * SW]
 
 
     def b0(s, d, sem):
@@ -342,8 +347,7 @@
     events.sort(key=lambda e: e[0])
 
     def step(n, _):
-        for e in range(2):
-            select(n // 2, (n % 2) * 2 + e)
+        select(n // 2, n % 2)
         for k in range(8):
             now = [run for time, run in events if 2 * k + 1.5 <= time < 2 * k + 3.5]
             if now:

time: 100 us -> 97.2 us (0.972)
  Pallas kernels: 98.2 us -> 95.3 us
    pallas_call x1, Pallas kernels: 13.2 us -> 11 us  [spectrum(): pl.pallas_call(spectrum_kernel, out_shape=jax.ShapeDtypeStruct((8, 256, 2...]
where the time goes in v6:
time: 97.2 us; the launch traced here: 97 us
  Pallas kernels  95.3 us (98%)
  local copies, waits for them, and re-layouts  1.54 us (2%)
    pallas_call x1, Pallas kernels, exchange(): pl.pallas_call(exchange_kernel, out_shape=(jax.ShapeDtypeStruct((COLS, GA...  78.2 us
    pallas_call x1, Pallas kernels, spectrum(): pl.pallas_call(spectrum_kernel, out_shape=jax.ShapeDtypeStruct((8, 256, 2...  11 us
    pallas_call x1, Pallas kernels, contract(): pl.pallas_call(response_kernel, out_shape=jax.ShapeDtypeStruct((2, GA, GB...  6.05 us

profile of v6, /device:TPU:0, one launch (start us, length us, event | category | flops | bytes accessed | tf_op | source)
XLA Modules:
  0.0 97.0 jit_solution(13285736174167265021)
XLA Ops:
  0.0 0.0 copy-start
  0.0 0.9 reshape.3.index_ref
  0.9 0.0 copy-start.1
  0.9 0.7 copy-done.1
  1.6 11.0 %spectrum.1.xt = bf16[8,256,256]{2,1,0:T(8,128)(2,1)S(1)} custom-call(s32[2,8]{1,0:T(2,128)S(1)} %bitcast.1, f32[16]{0:T(128)} %v_hbm.1, f32[128]{0:T(128)} %c_hbm.1, bf16[2,16,32768]{2,1,0:T(8,128)(2,1)} %valence.1, bf16[2,128,32768]{2,1,0:T(8,128)(2,1)} %conduction.1, bf16[2,512,512]{2,1,0:T(8,128)(2,1)} %constant.8.clone.ta_hbm, ...), custom_call_target="tpu_custom_call" | custom-call | tf_op jit(solution)/shard_map/spectrum/pallas_call | solution.py:138
  12.6 0.0 copy-done
  12.6 78.2 %exchange.1 = (bf16[16,2048,128]{2,1,0:T(8,128)(2,1)S(1)}, bf16[2,2048,1024]{2,1,0:T(8,128)(2,1)S(1)}, f32[2,2,1536,512]{3,2,1,0:T(8,128)S(1)}) custom-call(bf16[8,256,256]{2,1,0:T(8,128)(2,1)S(1)} %spectrum.1.xt, s32[32,512]{1,0:T(8,128)S(1)} %reshape.3.index_ref, bf16[16,128]{1,0:T(8,128)(2,1)S(1)} %copy-done), custom_call_target="tpu_custom_call" | custom-call | tf_op jit(solution)/shard_map/exchange/pallas_call | solution.py:445
  90.8 6.1 %contract.1 = f32[2,2048,1024]{2,1,0:T(8,128)} custom-call(bf16[16,2048,128]{2,1,0:T(8,128)(2,1)S(1)} %get-tuple-element.8.a_ref, bf16[2,2048,1024]{2,1,0:T(8,128)(2,1)S(1)} %get-tuple-element.9.rhs, f32[2,2,1536,512]{3,2,1,0:T(8,128)S(1)} %get-tuple-element.10.part_ref), custom_call_target="tpu_custom_call" | custom-call | tf_op jit(solution)/shard_map/contract/pallas_call | solution.py:502
Async XLA Ops:
  0.0 12.6 %copy-start = (bf16[16,128]{1,0:T(8,128)(2,1)S(1)}, bf16[16,128]{1,0:T(8,128)(2,1)}, u32[]{:S(2)}) copy-start(bf16[16,128]{1,0:T(8,128)(2,1)} %constant.11.clone.fold_ref) | copy-start | bytes 12292
  0.9 0.7 copy-start.1

commit v7 on v6

--- a/solution.py
+++ b/solution.py
@@ -200,7 +200,7 @@
 
 
     def select(s, m):
-        k = jnp.concatenate([index_ref[pl.ds((4 * m + e) * SUB + place(s), 1), :] for e in range(4)], axis=1)
+        k = jnp.concatenate([index_ref[pl.ds(pl.multiple_of(((4 * m + e) * SUB + place(s)) * SW, SW), SW)].reshape(1, SW) for e in range(4)], axis=1)
         ka = (k >> 10) * 8 + ((k >> 5) & 7)
         kb = ((k >> 8) & 3) * 32 + (k & 31)
         hot = jnp.where(lax.broadcasted_iota(jnp.int32, (KA, GW), 0) == ka, 1.0, 0.0).astype(jnp.bfloat16)
@@ -466,7 +466,7 @@
             collective_id=0, has_side_effects=True, vmem_limit_bytes=24 << 20
         ),
         name="exchange",
-    )(xt, index.reshape(ROWS * SUB, SW), jnp.asarray(dft_tables()[3]))
+    )(xt, index, jnp.asarray(dft_tables()[3]))
 
 
 TAIL = 128

time: 97.2 us -> 96.3 us (level)
  no operation moved by 1% of the time
where the time goes in v7:
time: 96.3 us; the launch traced here: 96.2 us
  Pallas kernels  95.3 us (99%)
    pallas_call x1, Pallas kernels, exchange(): pl.pallas_call(exchange_kernel, out_shape=(jax.ShapeDtypeStruct((COLS, GA...  78.2 us
    pallas_call x1, Pallas kernels, spectrum(): pl.pallas_call(spectrum_kernel, out_shape=jax.ShapeDtypeStruct((8, 256, 2...  11.1 us
    pallas_call x1, Pallas kernels, contract(): pl.pallas_call(response_kernel, out_shape=jax.ShapeDtypeStruct((2, GA, GB...  6.05 us

profile of v7, /device:TPU:0, one launch (start us, length us, event | category | flops | bytes accessed | tf_op | source)
XLA Modules:
  0.0 96.2 jit_solution(13148914214567047288)
XLA Ops:
  0.0 0.0 copy-start.1
  0.0 0.0 copy-start
  0.0 0.0 copy-start.2
  0.0 0.7 copy-done.2
  0.7 11.1 %spectrum.1.xt = bf16[8,256,256]{2,1,0:T(8,128)(2,1)S(1)} custom-call(s32[2,8]{1,0:T(2,128)S(1)} %bitcast.1, f32[16]{0:T(128)} %v_hbm.1, f32[128]{0:T(128)} %c_hbm.1, bf16[2,16,32768]{2,1,0:T(8,128)(2,1)} %valence.1, bf16[2,128,32768]{2,1,0:T(8,128)(2,1)} %conduction.1, bf16[2,512,512]{2,1,0:T(8,128)(2,1)} %constant.8.clone.ta_hbm, ...), custom_call_target="tpu_custom_call" | custom-call | tf_op jit(solution)/shard_map/spectrum/pallas_call | solution.py:138
  11.8 0.0 copy-done.1
  11.8 0.0 copy-done
  11.8 78.2 %exchange.1 = (bf16[16,2048,128]{2,1,0:T(8,128)(2,1)S(1)}, bf16[2,2048,1024]{2,1,0:T(8,128)(2,1)S(1)}, f32[2,2,1536,512]{3,2,1,0:T(8,128)S(1)}) custom-call(bf16[8,256,256]{2,1,0:T(8,128)(2,1)S(1)} %spectrum.1.xt, s32[16384]{0:T(1024)S(1)} %copy-done, bf16[16,128]{1,0:T(8,128)(2,1)S(1)} %copy-done.1), custom_call_target="tpu_custom_call" | custom-call | tf_op jit(solution)/shard_map/exchange/pallas_call | solution.py:445
  90.0 6.1 %contract.1 = f32[2,2048,1024]{2,1,0:T(8,128)} custom-call(bf16[16,2048,128]{2,1,0:T(8,128)(2,1)S(1)} %get-tuple-element.8.a_ref, bf16[2,2048,1024]{2,1,0:T(8,128)(2,1)S(1)} %get-tuple-element.9.rhs, f32[2,2,1536,512]{3,2,1,0:T(8,128)S(1)} %get-tuple-element.10.part_ref), custom_call_target="tpu_custom_call" | custom-call | tf_op jit(solution)/shard_map/contract/pallas_call | solution.py:502
Async XLA Ops:
  0.0 11.8 %copy-start.1 = (bf16[16,128]{1,0:T(8,128)(2,1)S(1)}, bf16[16,128]{1,0:T(8,128)(2,1)}, u32[]{:S(2)}) copy-start(bf16[16,128]{1,0:T(8,128)(2,1)} %constant.11.clone.fold_ref) | copy-start | bytes 12292
  0.0 11.8 %copy-start = (s32[16384]{0:T(1024)S(1)}, s32[16384]{0:T(1024)}, u32[]{:S(2)}) copy-start(s32[16384]{0:T(1024)} %index_ref.1) | copy-start | bytes 196612
  0.0 0.7 copy-start.2
